TPU v7x, 1024 devices: a whole 8x8x8 slice. The times are simulated.
1024 devices in a mesh: gx: 16 (over z, core), gy: 16 (over y, x_hi), gz: 4 (over x_lo).
Axes of the slice: x: 8 (x_hi: 2, x_lo: 4; x = x_hi * 4 + x_lo), y: 8, z: 8, core: 2. Of those that a mesh axis runs over, the one named last changes fastest.
Arguments:
- spacetime: float32 [22, 64, 64, 512], P(None, 'gx', 'gy', 'gz'), may hold values from -0.2 to 1.12, as said below
- fluid: float32 [8, 64, 64, 512], P(None, 'gx', 'gy', 'gz'), may hold values from -20 to 20, as said below
Outputs:
- spacetime_next: float32 [22, 64, 64, 512], P(None, 'gx', 'gy', 'gz')
- fluid_next: float32 [8, 64, 64, 512], P(None, 'gx', 'gy', 'gz')
Inputs may be any that keep to these rules, and one draw needn't show every extreme that they name: `spacetime`: chi and the lapse are positive and at most one; the conformal metric's entries are each within 0.12 of those of the identity. `fluid`: the first five components are densitized conserved values of states with positive density and pressure and speeds below one; the face fields have zero discrete divergence up to rounding.
All inputs are finite; a program needn't handle non-finite values.
Results may differ from a plain program's by a relative error of at most 0.0003.
Values sent between devices are 32-bit elements; how exact they have to be, the bound alone decides.
A program may use at most 32 MiB of HBM per device.

v0:
```python
import math

import jax
import jax.numpy as jnp
from jax import lax
from jax.sharding import PartitionSpec as P

GHOST = 3
RECOVERY_STEPS = 4


INDEX_PAIRS = ((0, 0), (0, 1), (0, 2), (1, 1), (1, 2), (2, 2))
FIRST_WEIGHTS = ((-2, 1.0 / 12.0), (-1, -8.0 / 12.0), (1, 8.0 / 12.0), (2, -1.0 / 12.0))
SECOND_WEIGHTS = (
    (-2, -1.0 / 12.0),
    (-1, 16.0 / 12.0),
    (0, -30.0 / 12.0),
    (1, 16.0 / 12.0),
    (2, -1.0 / 12.0),
)
KREISS_WEIGHTS = (
    (-3, 1.0 / 64.0),
    (-2, -6.0 / 64.0),
    (-1, 15.0 / 64.0),
    (0, -20.0 / 64.0),
    (1, 15.0 / 64.0),
    (2, -6.0 / 64.0),
    (3, 1.0 / 64.0),
)
COURANT = 0.25
DISSIPATION = 0.2
KAPPA_ONE = 0.02
SHIFT_DAMPING = 1.0
SPEED_CAP = 0.99
PRESSURE_FLOOR = 0.01
FOUR_PI = 4.0 * math.pi


def with_halo(cells, sides, width):
    for axis, dim in sides:
        count = lax.axis_size(axis)
        head = lax.slice_in_dim(cells, 0, width, axis=dim)
        tail = lax.slice_in_dim(cells, cells.shape[dim] - width, cells.shape[dim], axis=dim)
        cells = jnp.concatenate(
            [
                lax.ppermute(tail, axis, [(i, (i + 1) % count) for i in range(count)]),
                cells,
                lax.ppermute(head, axis, [((i + 1) % count, i) for i in range(count)]),
            ],
            axis=dim,
        )
    return cells


def add_all(pieces):
    summed = pieces[0]
    for member in pieces[1:]:
        summed = summed + member
    return summed


def inner_three(first_vec, second_vec):
    return add_all([first_vec[i] * second_vec[i] for i in range(3)])


def pair_slot(i, j):
    return INDEX_PAIRS.index((min(i, j), max(i, j)))


def symmetric(stack, offset):
    return [[stack[offset + pair_slot(i, j)] for j in range(3)] for i in range(3)]


def full_matrix(table):
    return [[table[min(i, j), max(i, j)] for j in range(3)] for i in range(3)]


def others(direction):
    return [b for b in range(3) if b != direction]


def window(values, direction, low_cut, high_cut):
    position = values.ndim - 3 + direction
    return lax.slice_in_dim(values, low_cut, values.shape[position] - high_cut, axis=position)


def interior(values, directions):
    for direction in directions:
        values = window(values, direction, GHOST, GHOST)
    return values


def stencil(values, direction, weights):
    summed = None
    for offset, weight in weights:
        term_value = weight * window(values, direction, GHOST + offset, GHOST - offset)
        summed = term_value if summed is None else summed + term_value
    return summed


def first_derivs(padded):
    return [stencil(interior(padded, others(a)), a, FIRST_WEIGHTS) for a in range(3)]


def second_derivs(padded):
    result = {}
    for a in range(3):
        for b in range(a, 3):
            if a == b:
                result[a, b] = stencil(interior(padded, others(a)), a, SECOND_WEIGHTS)
            else:
                remaining = [c for c in range(3) if c != a and c != b]
                result[a, b] = stencil(
                    stencil(interior(padded, remaining), a, FIRST_WEIGHTS), b, FIRST_WEIGHTS
                )
    return result


def dissipation(padded):
    summed = stencil(interior(padded, others(0)), 0, KREISS_WEIGHTS)
    for a in (1, 2):
        summed = summed + stencil(interior(padded, others(a)), a, KREISS_WEIGHTS)
    return DISSIPATION * summed


def inverse_metric(metric):
    cofactor = {}
    cofactor[0, 0] = metric[1][1] * metric[2][2] - metric[1][2] * metric[1][2]
    cofactor[0, 1] = metric[0][2] * metric[1][2] - metric[0][1] * metric[2][2]
    cofactor[0, 2] = metric[0][1] * metric[1][2] - metric[0][2] * metric[1][1]
    cofactor[1, 1] = metric[0][0] * metric[2][2] - metric[0][2] * metric[0][2]
    cofactor[1, 2] = metric[0][1] * metric[0][2] - metric[0][0] * metric[1][2]
    cofactor[2, 2] = metric[0][0] * metric[1][1] - metric[0][1] * metric[0][1]
    determinant = (
        metric[0][0] * cofactor[0, 0]
        + metric[0][1] * cofactor[0, 1]
        + metric[0][2] * cofactor[0, 2]
    )
    return full_matrix({pair: cofactor[pair] / determinant for pair in INDEX_PAIRS})


def wave_speed(current):
    inverse = inverse_metric(symmetric(current, 1))
    speeds = [
        jnp.abs(current[8 + d]) + jnp.sqrt(2.0 * current[7] * current[0] * inverse[d][d])
        for d in range(3)
    ]
    return jnp.maximum(jnp.maximum(speeds[0], speeds[1]), speeds[2])


def stress_parts(rest_mass, pressure, four_vel, magnetic):
    lorentz = jnp.sqrt(1.0 + inner_three(four_vel, four_vel))
    velocity = [four_vel[i] / lorentz for i in range(3)]
    along_b = inner_three(velocity, magnetic)
    time_b = lorentz * along_b
    space_b = [magnetic[i] / lorentz + time_b * velocity[i] for i in range(3)]
    b_square = inner_three(magnetic, magnetic) / (lorentz * lorentz) + along_b * along_b
    enthalpy = rest_mass + 2.0 * pressure
    inertia = enthalpy + b_square
    total_pressure = pressure + 0.5 * b_square
    return (lorentz, velocity, time_b, space_b, b_square, enthalpy, inertia, total_pressure)


def face_state(rest_mass, pressure, four_vel, magnetic, d):
    lorentz, velocity, time_b, space_b, b_square, enthalpy, inertia, total_pressure = stress_parts(
        rest_mass, pressure, four_vel, magnetic
    )
    lorentz_sq = lorentz * lorentz
    density = rest_mass * lorentz
    conserved = [density] + [
        inertia * lorentz_sq * velocity[j] - time_b * space_b[j] for j in range(3)
    ]
    conserved = conserved + [inertia * lorentz_sq - total_pressure - time_b * time_b - density]
    flux_list = [density * velocity[d]]
    for j in range(3):
        flux_j = inertia * lorentz_sq * velocity[d] * velocity[j] - space_b[d] * space_b[j]
        if j == d:
            flux_j = flux_j + total_pressure
        flux_list.append(flux_j)
    flux_list.append(
        inertia * lorentz_sq * velocity[d] - time_b * space_b[d] - density * velocity[d]
    )
    speed_sq = inner_three(velocity, velocity)
    sound_sq = 2.0 * pressure / enthalpy
    alfven_sq = b_square / inertia
    fast_sq = sound_sq + alfven_sq - sound_sq * alfven_sq
    spread = jnp.sqrt(
        fast_sq
        * (1.0 - speed_sq)
        * (1.0 - speed_sq * fast_sq - velocity[d] * velocity[d] * (1.0 - fast_sq))
    )
    middle = velocity[d] * (1.0 - fast_sq)
    fastest = jnp.maximum(jnp.abs(middle + spread), jnp.abs(middle - spread)) / (
        1.0 - speed_sq * fast_sq
    )
    return (conserved, flux_list, fastest)


def recover(conserved, magnetic):
    density = conserved[0]
    momenta = [conserved[1 + i] for i in range(3)]
    energy = conserved[4] + density
    mom_sq = inner_three(momenta, momenta)
    mag_sq = inner_three(magnetic, magnetic)
    cross = inner_three(momenta, magnetic)
    cross_sq = cross * cross

    def recovered_state(guess_z):
        speed_sq = (mom_sq * guess_z * guess_z + cross_sq * (2.0 * guess_z + mag_sq)) / (
            guess_z * guess_z * (guess_z + mag_sq) * (guess_z + mag_sq)
        )
        inv_lorentz_sq = 1.0 - jnp.minimum(speed_sq, SPEED_CAP)
        rest_mass = density * jnp.sqrt(inv_lorentz_sq)
        pressure = 0.5 * (guess_z * inv_lorentz_sq - rest_mass)
        return (inv_lorentz_sq, rest_mass, pressure)

    guess_z = jnp.maximum(energy - 0.5 * mag_sq, density)
    for attempt in range(RECOVERY_STEPS):
        inv_lorentz_sq, rest_mass, pressure = recovered_state(guess_z)
        residual = (
            guess_z
            + mag_sq
            - pressure
            - 0.5 * mag_sq * inv_lorentz_sq
            - 0.5 * cross_sq / (guess_z * guess_z)
            - energy
        )
        guess_z = jnp.maximum(guess_z - residual / (1.0 - 0.5 * inv_lorentz_sq), density)
    inv_lorentz_sq, rest_mass, pressure = recovered_state(guess_z)
    pressure = jnp.maximum(pressure, PRESSURE_FLOOR * rest_mass)
    lorentz = 1.0 / jnp.sqrt(inv_lorentz_sq)
    four_vel = [
        lorentz * (momenta[i] + cross * magnetic[i] / guess_z) / (guess_z + mag_sq)
        for i in range(3)
    ]
    return (rest_mass, pressure, four_vel)


def limited(low_side, high_side):
    return (
        0.5
        * (jnp.sign(low_side) + jnp.sign(high_side))
        * jnp.minimum(jnp.abs(low_side), jnp.abs(high_side))
    )


def corner_box(values):
    for direction in range(3):
        values = window(values, direction, 0, 1)
    return values


def owned_box(values):
    for direction in range(3):
        values = window(values, direction, GHOST, GHOST - 1)
    return values


def edge_cells(values):
    for direction in range(3):
        values = window(values, direction, GHOST - 1, 1)
    return values


def face_average(values, d):
    paired = window(values, d, GHOST - 1, GHOST - 1)
    return interior(0.5 * (window(paired, d, 0, 1) + window(paired, d, 1, 0)), others(d))


def edge_average(values, d):
    values = window(values, d, 1, 1)
    for e in others(d):
        values = 0.5 * (window(values, e, 0, 1) + window(values, e, 1, 0))
    return values


def edge_difference(edge_vals, d, e):
    edge_vals = window(edge_vals, d, 0, 1)
    return window(edge_vals, e, 1, 0) - window(edge_vals, e, 0, 1)


def fluid_rates(padded_st, padded_fl, current, gradient):
    chi_box = corner_box(padded_st[0])
    volume_box = 1.0 / (chi_box * jnp.sqrt(chi_box))
    centred = []
    for d in range(3):
        averaged = 0.5 * (window(padded_fl[5 + d], d, 0, 1) + window(padded_fl[5 + d], d, 1, 0))
        for e in others(d):
            averaged = window(averaged, e, 0, 1)
        centred.append(averaged)
    magnetic_box = [centred[d] / volume_box for d in range(3)]
    conserved_box = corner_box(padded_fl[:5]) / volume_box
    rest_mass, pressure, four_vel = recover(conserved_box, magnetic_box)
    primitives = jnp.stack([rest_mass, pressure] + four_vel + magnetic_box)
    hydro_rate = [0.0] * 5
    for d in range(3):
        line_prims = window(primitives, d, 1, 0)
        for e in others(d):
            line_prims = window(line_prims, e, GHOST, GHOST - 1)
        low_diff = window(line_prims, d, 1, 1) - window(line_prims, d, 0, 2)
        high_diff = window(line_prims, d, 2, 0) - window(line_prims, d, 1, 1)
        slopes = limited(low_diff, high_diff)
        centre = window(line_prims, d, 1, 1)
        left_state = window(centre, d, 0, 1) + 0.5 * window(slopes, d, 0, 1)
        right_state = window(centre, d, 1, 0) - 0.5 * window(slopes, d, 1, 0)
        lapse_face = face_average(padded_st[7], d)
        chi_face = face_average(padded_st[0], d)
        volume_face = 1.0 / (chi_face * jnp.sqrt(chi_face))
        normal = interior(window(padded_fl[5 + d], d, GHOST, GHOST - 1), others(d)) / volume_face
        fluxes = []
        for one_side in (left_state, right_state):
            magnetic = [one_side[5 + i] for i in range(3)]
            magnetic[d] = normal
            fluxes.append(
                face_state(
                    one_side[0], one_side[1], [one_side[2], one_side[3], one_side[4]], magnetic, d
                )
            )
        cons_left, flux_left, fast_left = fluxes[0]
        cons_right, flux_right, fast_right = fluxes[1]
        signal = jnp.maximum(fast_left, fast_right)
        weight = lapse_face * volume_face
        for q in range(5):
            face_flux = weight * (
                0.5 * (flux_left[q] + flux_right[q]) - 0.5 * signal * (cons_right[q] - cons_left[q])
            )
            hydro_rate[q] = hydro_rate[q] - (
                window(face_flux, d, 1, 0) - window(face_flux, d, 0, 1)
            )
    owned_prims = owned_box(primitives)
    lorentz, velocity, time_b, space_b, b_square, enthalpy, inertia, total_pressure = stress_parts(
        owned_prims[0],
        owned_prims[1],
        [owned_prims[2], owned_prims[3], owned_prims[4]],
        [owned_prims[5], owned_prims[6], owned_prims[7]],
    )
    lorentz_sq = lorentz * lorentz
    stress_pairs = {}
    for i, j in INDEX_PAIRS:
        stress_ij = inertia * lorentz_sq * velocity[i] * velocity[j] - space_b[i] * space_b[j]
        if i == j:
            stress_ij = stress_ij + total_pressure
        stress_pairs[i, j] = stress_ij
    stress = full_matrix(stress_pairs)
    held = interior(padded_fl[:5], (0, 1, 2))
    conformal = current[0]
    volume = 1.0 / (conformal * jnp.sqrt(conformal))
    lapse_now = current[7]
    lapse_grad = [gradient[k][7] for k in range(3)]
    trace_total = current[11] + 2.0 * current[21]
    metric = symmetric(current, 1)
    traceless = symmetric(current, 12)
    curv_phys = full_matrix(
        {
            pair: (traceless[pair[0]][pair[1]] + metric[pair[0]][pair[1]] * trace_total / 3.0)
            / conformal
            for pair in INDEX_PAIRS
        }
    )
    total_energy = held[4] + held[0]
    for i in range(3):
        hydro_rate[1 + i] = (
            hydro_rate[1 + i]
            - total_energy * lapse_grad[i]
            + add_all([held[1 + k] * gradient[i][8 + k] for k in range(3)])
        )
    hydro_rate[4] = (
        hydro_rate[4]
        + lapse_now
        * volume
        * add_all([stress[i][j] * curv_phys[i][j] for i in range(3) for j in range(3)])
        - add_all([held[1 + j] * lapse_grad[j] for j in range(3)])
    )
    matter = {
        "energy": total_energy / volume,
        "momentum": [held[1 + i] / volume for i in range(3)],
        "stress": stress,
    }
    four_edge = [edge_cells(four_vel[i]) for i in range(3)]
    lorentz_edge = jnp.sqrt(1.0 + inner_three(four_edge, four_edge))
    vel_edge = [four_edge[i] / lorentz_edge for i in range(3)]
    mag_edge = [edge_cells(centred[i]) for i in range(3)]
    lapse_cells = padded_st[7]
    for direction in range(3):
        lapse_cells = window(lapse_cells, direction, GHOST - 1, GHOST - 1)
    electric = [
        -lapse_cells
        * (
            vel_edge[(i + 1) % 3] * mag_edge[(i + 2) % 3]
            - vel_edge[(i + 2) % 3] * mag_edge[(i + 1) % 3]
        )
        for i in range(3)
    ]
    edge_vals = [edge_average(electric[i], i) for i in range(3)]
    field_rate = []
    for d in range(3):
        e = (d + 1) % 3
        f = (d + 2) % 3
        field_rate.append(
            -(edge_difference(edge_vals[f], d, e) - edge_difference(edge_vals[e], d, f))
        )
    return (hydro_rate, field_rate, matter)


def z4c_rates(padded_st, current, gradient, matter):
    curvature = second_derivs(padded_st[:11])

    def hessian(field, a, b):
        return curvature[min(a, b), max(a, b)][field]

    conformal = current[0]
    metric = symmetric(current, 1)
    lapse_now = current[7]
    shift_vec = [current[8 + i] for i in range(3)]
    extrinsic = current[11]
    traceless = symmetric(current, 12)
    connection = [current[18 + i] for i in range(3)]
    z_theta = current[21]
    inverse = inverse_metric(metric)
    metric_grad = [
        [[gradient[k][1 + pair_slot(i, j)] for j in range(3)] for i in range(3)] for k in range(3)
    ]
    lowered = [
        [
            [
                0.5 * (metric_grad[j][i][k] + metric_grad[k][i][j] - metric_grad[i][j][k])
                for k in range(3)
            ]
            for j in range(3)
        ]
        for i in range(3)
    ]
    raised = [
        [
            [add_all([inverse[i][l] * lowered[l][j][k] for l in range(3)]) for k in range(3)]
            for j in range(3)
        ]
        for i in range(3)
    ]
    contracted = [
        add_all([inverse[j][k] * raised[i][j][k] for j in range(3) for k in range(3)])
        for i in range(3)
    ]
    chi_grad = [gradient[k][0] for k in range(3)]
    lapse_grad = [gradient[k][7] for k in range(3)]
    chi_cov = full_matrix(
        {
            pair: hessian(0, pair[0], pair[1])
            - add_all([raised[k][pair[0]][pair[1]] * chi_grad[k] for k in range(3)])
            for pair in INDEX_PAIRS
        }
    )
    chi_lap = add_all([inverse[i][j] * chi_cov[i][j] for i in range(3) for j in range(3)])
    chi_square = add_all(
        [inverse[i][j] * chi_grad[i] * chi_grad[j] for i in range(3) for j in range(3)]
    )
    cross_term = add_all(
        [inverse[i][j] * chi_grad[i] * lapse_grad[j] for i in range(3) for j in range(3)]
    )
    lapse_cov = full_matrix(
        {
            pair: hessian(7, pair[0], pair[1])
            - add_all([raised[k][pair[0]][pair[1]] * lapse_grad[k] for k in range(3)])
            + (
                chi_grad[pair[0]] * lapse_grad[pair[1]]
                + chi_grad[pair[1]] * lapse_grad[pair[0]]
                - metric[pair[0]][pair[1]] * cross_term
            )
            / (2.0 * conformal)
            for pair in INDEX_PAIRS
        }
    )
    lapse_lap = conformal * add_all(
        [inverse[i][j] * lapse_cov[i][j] for i in range(3) for j in range(3)]
    )
    ricci_pairs = {}
    for i, j in INDEX_PAIRS:
        slot_index = 1 + pair_slot(i, j)
        second_part = -0.5 * add_all(
            [inverse[l][m] * hessian(slot_index, l, m) for l in range(3) for m in range(3)]
        )
        connection_part = 0.5 * add_all(
            [
                metric[k][i] * gradient[j][18 + k] + metric[k][j] * gradient[i][18 + k]
                for k in range(3)
            ]
        )
        contracted_part = 0.5 * add_all(
            [contracted[k] * (lowered[i][j][k] + lowered[j][i][k]) for k in range(3)]
        )
        quadratic = add_all(
            [
                inverse[l][m]
                * (
                    raised[k][l][i] * lowered[j][k][m]
                    + raised[k][l][j] * lowered[i][k][m]
                    + raised[k][i][m] * lowered[k][l][j]
                )
                for l in range(3)
                for m in range(3)
                for k in range(3)
            ]
        )
        conformal_part = (chi_cov[i][j] + metric[i][j] * chi_lap) / (2.0 * conformal) - (
            chi_grad[i] * chi_grad[j] + 3.0 * metric[i][j] * chi_square
        ) / (4.0 * conformal * conformal)
        ricci_pairs[i, j] = (
            second_part + connection_part + contracted_part + quadratic + conformal_part
        )
    ricci_ten = full_matrix(ricci_pairs)
    ricci_scalar = conformal * add_all(
        [inverse[i][j] * ricci_ten[i][j] for i in range(3) for j in range(3)]
    )
    stress = matter["stress"]
    density_adm = matter["energy"]
    momentum = matter["momentum"]
    stress_trace = conformal * add_all(
        [inverse[i][j] * stress[i][j] for i in range(3) for j in range(3)]
    )
    raised_a = full_matrix(
        {
            pair: add_all(
                [
                    inverse[pair[0]][k] * inverse[pair[1]][l] * traceless[k][l]
                    for k in range(3)
                    for l in range(3)
                ]
            )
            for pair in INDEX_PAIRS
        }
    )
    a_square = add_all([traceless[i][j] * raised_a[i][j] for i in range(3) for j in range(3)])
    shift_grad = [[gradient[k][8 + i] for i in range(3)] for k in range(3)]
    shift_div = add_all([shift_grad[k][k] for k in range(3)])
    trace_total = extrinsic + 2.0 * z_theta

    def advect(field):
        return add_all([shift_vec[k] * gradient[k][field] for k in range(3)])

    rate_list = [None] * current.shape[0]
    rate_list[0] = advect(0) + 2.0 / 3.0 * conformal * (lapse_now * trace_total - shift_div)
    rate_list[7] = advect(7) - 2.0 * lapse_now * extrinsic
    for i in range(3):
        rate_list[8 + i] = advect(8 + i) + 0.75 * connection[i] - SHIFT_DAMPING * shift_vec[i]
    rate_list[11] = (
        advect(11)
        - lapse_lap
        + lapse_now * (a_square + trace_total * trace_total / 3.0)
        + FOUR_PI * lapse_now * (stress_trace + density_adm)
        + KAPPA_ONE * lapse_now * z_theta
    )
    source = [
        [
            -lapse_cov[i][j] + lapse_now * (ricci_ten[i][j] - 2.0 * FOUR_PI * stress[i][j])
            for j in range(3)
        ]
        for i in range(3)
    ]
    source_trace = add_all([inverse[i][j] * source[i][j] for i in range(3) for j in range(3)])
    for i, j in INDEX_PAIRS:
        slot_index = pair_slot(i, j)
        rate_list[1 + slot_index] = (
            advect(1 + slot_index)
            + add_all(
                [
                    metric[i][k] * shift_grad[j][k] + metric[j][k] * shift_grad[i][k]
                    for k in range(3)
                ]
            )
            - 2.0 / 3.0 * metric[i][j] * shift_div
            - 2.0 * lapse_now * traceless[i][j]
        )
        product = add_all(
            [traceless[i][k] * inverse[k][l] * traceless[l][j] for k in range(3) for l in range(3)]
        )
        rate_list[12 + slot_index] = (
            advect(12 + slot_index)
            + add_all(
                [
                    traceless[i][k] * shift_grad[j][k] + traceless[j][k] * shift_grad[i][k]
                    for k in range(3)
                ]
            )
            - 2.0 / 3.0 * traceless[i][j] * shift_div
            + conformal * (source[i][j] - metric[i][j] * source_trace / 3.0)
            + lapse_now * (trace_total * traceless[i][j] - 2.0 * product)
        )
    for i in range(3):
        bracket = add_all([raised[i][j][k] * raised_a[j][k] for j in range(3) for k in range(3)])
        bracket = (
            bracket - 1.5 * add_all([raised_a[i][j] * chi_grad[j] for j in range(3)]) / conformal
        )
        bracket = (
            bracket
            - add_all([inverse[i][j] * (2.0 * gradient[j][11] + gradient[j][21]) for j in range(3)])
            / 3.0
        )
        bracket = bracket - 2.0 * FOUR_PI * add_all([inverse[i][j] * momentum[j] for j in range(3)])
        rate_list[18 + i] = (
            advect(18 + i)
            - add_all([contracted[j] * shift_grad[j][i] for j in range(3)])
            + 2.0 / 3.0 * contracted[i] * shift_div
            + add_all([inverse[j][k] * hessian(8 + i, j, k) for j in range(3) for k in range(3)])
            + add_all([inverse[i][j] * hessian(8 + k, j, k) for j in range(3) for k in range(3)])
            / 3.0
            - 2.0 * add_all([raised_a[i][j] * lapse_grad[j] for j in range(3)])
            + 2.0 * lapse_now * bracket
            - 2.0 * KAPPA_ONE * lapse_now * (connection[i] - contracted[i])
        )
    rate_list[21] = (
        advect(21)
        + 0.5
        * lapse_now
        * (
            ricci_scalar
            - a_square
            + 2.0 / 3.0 * trace_total * trace_total
            - 4.0 * FOUR_PI * density_adm
        )
        - 2.0 * KAPPA_ONE * lapse_now * z_theta
    )
    return jnp.stack(rate_list) + dissipation(padded_st)


def tendencies(padded_st, padded_fl):
    gradient = first_derivs(padded_st)
    current = interior(padded_st, (0, 1, 2))
    hydro_rate, field_rate, matter = fluid_rates(padded_st, padded_fl, current, gradient)
    spacetime_rate = z4c_rates(padded_st, current, gradient, matter)
    return (spacetime_rate, jnp.stack(hydro_rate + field_rate))


def per_device(spacetime, fluid):
    local_top = jnp.max(wave_speed(spacetime))
    fastest = lax.pmax(local_top, ("gx", "gy", "gz"))
    timestep = COURANT / fastest
    count_st = spacetime.shape[0]
    joined = jnp.concatenate((spacetime, fluid), axis=0)
    joined = with_halo(joined, (("gx", 1), ("gy", 2), ("gz", 3)), GHOST)
    padded_st = joined[:count_st]
    padded_fl = joined[count_st:]
    spacetime_rate, fluid_rate = tendencies(padded_st, padded_fl)
    return (spacetime + timestep * spacetime_rate, fluid + timestep * fluid_rate)


def solution(mesh):
    return jax.shard_map(
        per_device,
        mesh=mesh,
        in_specs=(P(None, "gx", "gy", "gz"), P(None, "gx", "gy", "gz")),
        out_specs=(P(None, "gx", "gy", "gz"), P(None, "gx", "gy", "gz")),
        check_vma=False,
    )
```

profile of v0, /device:TPU:1, one launch (start us, length us, event | category | flops | bytes accessed | tf_op | source)
XLA Modules:
  0.0 238.6 jit_solution(15344856532914170502)
XLA Ops:
  0.6 1.0 fusion.685
  1.6 0.9 fusion.690
  2.7 4.4 %collective-permute-start = (f32[30,3,4,128]{3,1,2,0:T(4,128)S(1)}, f32[30,3,4,128]{3,1,2,0:T(4,128)S(1)}, u32[]{:S(2)}, u32[]{:S(2)}) collective-permute-start(f32[30,3,4,128]{3,1,2,0:T(4,128)S(1)} %get-tuple-element.156), channel_id=1, source_target_pairs={{0,64},{64,128},{128,192},{192,256},{256,320},{320,384},{384,448},... | collective-permute-start | bytes 552968 | tf_op jit(solution)/shard_map/ppermute | solution.py:46
  7.1 9.8 %collective-permute-start.1 = (f32[30,3,4,128]{3,1,2,0:T(4,128)S(1)}, f32[30,3,4,128]{3,1,2,0:T(4,128)S(1)}, u32[]{:S(2)}, u32[]{:S(2)}) collective-permute-start(f32[30,3,4,128]{3,1,2,0:T(4,128)S(1)} %get-tuple-element.157), channel_id=1, source_target_pairs={{64,0},{128,64},{192,128},{256,192},{320,256},{384,320},{448,384},... | collective-permute-start | bytes 552968 | tf_op jit(solution)/shard_map/ppermute | solution.py:48
  16.8 1.0 collective-permute-done
  18.5 1.9 collective-permute-start.2
  20.6 9.4 %collective-permute-start.3 = (f32[30,10,3,128]{3,0,2,1:T(8,128)S(1)}, f32[30,10,3,128]{3,0,2,1:T(8,128)}, u32[]{:S(2)}, u32[]{:S(2)}) collective-permute-start(f32[30,10,3,128]{3,0,2,1:T(8,128)S(1)} %copy.59), channel_id=1, source_target_pairs={{4,0},{8,4},{12,8},{16,12},{20,16},{24,20},{28,24},{32,28},{36,32}... | collective-permute-start | bytes 1382408 | tf_op jit(solution)/shard_map/ppermute | solution.py:48
  30.6 149.2 %pmax.7 = f32[]{:T(128)} all-reduce(f32[]{:T(128)} %fusion.578), channel_id=1, replica_groups=mesh['gx'=16,'gy'=16,'gz'=4] {'gx','gy','gz'}, use_global_device_ids=true, to_apply=%region_1.0 | all-reduce | flops 1 | bytes 8 | tf_op jit(solution)/shard_map/pmax | solution.py:635
  180.6 1.0 multiply_add_fusion.3
  181.6 0.8 fusion.93
  182.7 1.3 copy.60
  184.5 3.0 %fusion.682 = (f32[30,10,10,3]{3,1,2,0:T(8,128)}, f32[30,10,10,3]{3,1,2,0:T(8,128)}) fusion(f32[30,10,10,128]{3,1,2,0:T(8,128)S(1)} %pad_maximum_fusion.1), kind=kLoop, calls=%fused_computation.1288 | loop fusion | bytes 144000 | tf_op jit(solution)/shard_map/slice | solution.py:43
  187.5 2.7 %copy.63 = f32[30,10,10,3]{0,3,2,1:T(4,128)S(1)} copy(f32[30,10,10,3]{3,1,2,0:T(8,128)} %get-tuple-element.139) | data formatting | bytes 72000 | tf_op jit(solution)/shard_map/slice | solution.py:43
  190.2 2.7 %collective-permute-start.4 = (f32[30,10,10,3]{0,3,2,1:T(4,128)S(1)}, f32[30,10,10,3]{0,3,2,1:T(4,128)}, u32[]{:S(2)}, u32[]{:S(2)}) collective-permute-start(f32[30,10,10,3]{0,3,2,1:T(4,128)S(1)} %copy.63), channel_id=1, source_target_pairs={{0,1},{1,2},{2,3},{3,0},{4,5},{5,6},{6,7},{7,4},{8,9},{9,10},{10,1... | collective-permute-start | bytes 108008 | tf_op jit(solution)/shard_map/ppermute | solution.py:46
  192.9 3.4 %copy.65 = f32[30,10,10,3]{0,3,2,1:T(4,128)} copy(f32[30,10,10,3]{3,1,2,0:T(8,128)} %get-tuple-element.140) | data formatting | bytes 72000 | tf_op jit(solution)/shard_map/slice | solution.py:42
  196.3 4.6 %collective-permute-start.5 = (f32[30,10,10,3]{0,3,2,1:T(4,128)}, f32[30,10,10,3]{0,3,2,1:T(4,128)}, u32[]{:S(2)}, u32[]{:S(2)}) collective-permute-start(f32[30,10,10,3]{0,3,2,1:T(4,128)} %copy.65), channel_id=1, source_target_pairs={{1,0},{2,1},{3,2},{0,3},{5,4},{6,5},{7,6},{4,7},{9,8},{10,9},{11,1... | collective-permute-start | bytes 108008 | tf_op jit(solution)/shard_map/ppermute | solution.py:48
  201.3 0.7 fusion.117
  202.0 0.8 fusion.110
  202.8 1.1 multiply_add_fusion.2
  203.9 3.0 %copy.64 = f32[30,10,10,3]{3,1,2,0:T(8,128)S(1)} copy(f32[30,10,10,3]{0,3,2,1:T(4,128)} %collective-permute-done.4) | data formatting | bytes 72000 | tf_op jit(solution)/shard_map/ppermute | solution.py:46
  207.0 4.3 %copy.66 = f32[30,10,10,3]{3,1,2,0:T(8,128)} copy(f32[30,10,10,3]{0,3,2,1:T(4,128)} %collective-permute-done.5) | data formatting | bytes 72000 | tf_op jit(solution)/shard_map/ppermute | solution.py:48
  211.2 1.3 maximum_bitcast_fusion
  214.1 4.3 %pad_maximum_fusion = f32[30,10,10,134]{3,1,2,0:T(8,128)S(1)} fusion(f32[30,10,10,3]{3,1,2,0:T(8,128)S(1)} %copy-done, f32[30,10,3,128]{3,1,2,0:T(8,128)S(1)} %copy-done.2, f32[30,3,4,128]{3,1,2,0:T(4,128)S(1)} %copy-done.6, f32[30,4,4,128]{3,1,2,0:T(4,128)S(1)} %get-tuple-element.174, f32[30,3,4,128]{3,1,2,0:T(4,128)S(1)} %copy-done.4, ...), kind=kLoop, calls=%fused_computation | loop fusion | flops 2412000 | bytes 3216000 | tf_op jit(solution)/shard_map/concatenate | solution.py:44
  218.5 1.0 constant_dynamic-update-slice_fusion.31
  224.0 1.6 multiply_add_fusion.1
  226.4 0.6 copy.90
  227.3 1.4 fusion.39
  228.7 1.1 fusion.36
  230.5 0.8 fusion.103
  231.8 1.4 constant_dynamic-update-slice_fusion.11
  234.1 3.8 %fusion.13 = f32[22,4,4,128]{3,1,2,0:T(4,128)S(1)} fusion(f32[22,4,4,128]{3,1,2,0:T(4,128)S(1)} %constant_dynamic-update-slice_fusion.2, f32[30,10,10,3]{3,1,2,0:T(8,128)S(1)} %copy-done, f32[30,10,3,128]{3,1,2,0:T(8,128)S(1)} %copy-done.2, f32[30,10,3,128]{3,1,2,0:T(8,128)S(1)} %copy.58, f32[30,3,4,128]{3,1,2,0:T(4,128)S(1)} %copy-done.6, ...), kind=kLoop, calls=%fused_computation.49 | loop fusion | flops 4370432 | bytes 2148676 | tf_op jit(solution)/shard_map/add | solution.py:643
  237.9 0.7 copy.89
  (128 shorter events, 11.6 us)
Async XLA Ops:
  1.6 200.3 %copy-start.7 = (f32[22,4,4,128]{3,1,2,0:T(4,128)}, f32[22,4,4,128]{3,1,2,0:T(4,128)S(1)}, u32[]{:S(2)}) copy-start(f32[22,4,4,128]{3,1,2,0:T(4,128)S(1)} %get-tuple-element.160) | copy-start | bytes 540676
  2.7 15.1 %collective-permute-start = (f32[30,3,4,128]{3,1,2,0:T(4,128)S(1)}, f32[30,3,4,128]{3,1,2,0:T(4,128)S(1)}, u32[]{:S(2)}, u32[]{:S(2)}) collective-permute-start(f32[30,3,4,128]{3,1,2,0:T(4,128)S(1)} %get-tuple-element.156), channel_id=1, source_target_pairs={{0,64},{64,128},{128,192},{192,256},{256,320},{320,384},{384,448},... | collective-permute-start | bytes 552968 | tf_op jit(solution)/shard_map/ppermute | solution.py:46
  7.1 10.9 %collective-permute-start.1 = (f32[30,3,4,128]{3,1,2,0:T(4,128)S(1)}, f32[30,3,4,128]{3,1,2,0:T(4,128)S(1)}, u32[]{:S(2)}, u32[]{:S(2)}) collective-permute-start(f32[30,3,4,128]{3,1,2,0:T(4,128)S(1)} %get-tuple-element.157), channel_id=1, source_target_pairs={{64,0},{128,64},{192,128},{256,192},{320,256},{384,320},{448,384},... | collective-permute-start | bytes 552968 | tf_op jit(solution)/shard_map/ppermute | solution.py:48
  17.8 185.0 %copy-start.3 = (f32[30,3,4,128]{3,1,2,0:T(4,128)}, f32[30,3,4,128]{3,1,2,0:T(4,128)S(1)}, u32[]{:S(2)}) copy-start(f32[30,3,4,128]{3,1,2,0:T(4,128)S(1)} %collective-permute-done) | copy-start | bytes 552964
  18.0 184.8 %copy-start.5 = (f32[30,3,4,128]{3,1,2,0:T(4,128)}, f32[30,3,4,128]{3,1,2,0:T(4,128)S(1)}, u32[]{:S(2)}) copy-start(f32[30,3,4,128]{3,1,2,0:T(4,128)S(1)} %collective-permute-done.1) | copy-start | bytes 552964
  18.5 163.9 %collective-permute-start.2 = (f32[30,10,3,128]{3,0,2,1:T(8,128)S(1)}, f32[30,10,3,128]{3,0,2,1:T(8,128)S(1)}, u32[]{:S(2)}, u32[]{:S(2)}) collective-permute-start(f32[30,10,3,128]{3,0,2,1:T(8,128)S(1)} %copy.57), channel_id=1, source_target_pairs={{0,4},{4,8},{8,12},{12,16},{16,20},{20,24},{24,28},{28,32},{32,36}... | collective-permute-start | bytes 1382408 | tf_op jit(solution)/shard_map/ppermute | solution.py:46
  20.6 162.1 %collective-permute-start.3 = (f32[30,10,3,128]{3,0,2,1:T(8,128)S(1)}, f32[30,10,3,128]{3,0,2,1:T(8,128)}, u32[]{:S(2)}, u32[]{:S(2)}) collective-permute-start(f32[30,10,3,128]{3,0,2,1:T(8,128)S(1)} %copy.59), channel_id=1, source_target_pairs={{4,0},{8,4},{12,8},{16,12},{20,16},{24,20},{28,24},{32,28},{36,32}... | collective-permute-start | bytes 1382408 | tf_op jit(solution)/shard_map/ppermute | solution.py:48
  184.1 18.8 %copy-start.1 = (f32[30,10,3,128]{3,1,2,0:T(8,128)}, f32[30,10,3,128]{3,1,2,0:T(8,128)S(1)}, u32[]{:S(2)}) copy-start(f32[30,10,3,128]{3,1,2,0:T(8,128)S(1)} %copy.60) | copy-start | bytes 1382404
  190.2 13.7 %collective-permute-start.4 = (f32[30,10,10,3]{0,3,2,1:T(4,128)S(1)}, f32[30,10,10,3]{0,3,2,1:T(4,128)}, u32[]{:S(2)}, u32[]{:S(2)}) collective-permute-start(f32[30,10,10,3]{0,3,2,1:T(4,128)S(1)} %copy.63), channel_id=1, source_target_pairs={{0,1},{1,2},{2,3},{3,0},{4,5},{5,6},{6,7},{7,4},{8,9},{9,10},{10,1... | collective-permute-start | bytes 108008 | tf_op jit(solution)/shard_map/ppermute | solution.py:46
  196.3 10.7 %collective-permute-start.5 = (f32[30,10,10,3]{0,3,2,1:T(4,128)}, f32[30,10,10,3]{0,3,2,1:T(4,128)}, u32[]{:S(2)}, u32[]{:S(2)}) collective-permute-start(f32[30,10,10,3]{0,3,2,1:T(4,128)} %copy.65), channel_id=1, source_target_pairs={{1,0},{2,1},{3,2},{0,3},{5,4},{6,5},{7,6},{4,7},{9,8},{10,9},{11,1... | collective-permute-start | bytes 108008 | tf_op jit(solution)/shard_map/ppermute | solution.py:48
  211.2 1.8 copy-start
  211.2 2.0 copy-start.2
  211.2 2.0 copy-start.4
  211.2 2.1 copy-start.6
  224.0 1.6 copy-start.8
  224.0 1.6 copy-start.9
  224.0 1.6 copy-start.10
  224.0 2.3 copy-start.15
  230.5 0.9 copy-start.12
  230.5 0.9 copy-start.13
  230.5 1.0 copy-start.14
  231.8 2.3 copy-start.11
where the time goes:
time: 239 us
  blocking collectives  149 us (62%)
  starting transfers between devices  32.7 us (14%)
  other arithmetic  30.6 us (13%)
  local copies, waits for them, and re-layouts  23 us (10%)
    pmax x1, blocking collectives, per_device(): fastest = lax.pmax(local_top, ('gx', 'gy', 'gz'))  149 us
    ppermute x3, starting transfers between devices, with_halo(): lax.ppermute(head, axis, [((i + 1) % count, i) for i in range(count)])  23.7 us
    add x11, other arithmetic, stencil(): summed = term_value if summed is None else summed + term_value  10.2 us
    ppermute x3, starting transfers between devices, with_halo(): lax.ppermute(tail, axis, [(i, (i + 1) % count) for i in range(count)])  8.97 us
    slice x5, local copies, waits for them, and re-layouts, with_halo(): lax.slice_in_dim(cells, cells.shape[dim] - width, cells.shape[dim], axis=...  6.14 us
    ppermute x2, local copies, waits for them, and re-layouts, with_halo(): lax.ppermute(head, axis, [((i + 1) % count, i) for i in range(count)])  5.58 us
    concatenate x3, other arithmetic, with_halo(): jnp.concatenate([lax.ppermute(tail, axis, [(i, (i + 1) % count) for i in...  4.95 us
    unnamed x32, other arithmetic  4.88 us
  transfers between devices with their start and end apart: 6, of which 2 were waited for; matrix products, arithmetic and copies ran while one was open for 5% of the time, Pallas kernels for 0%

commit v1 on v0

v1 whole, which is shorter than its diff:
```python
import math
import jax
import jax.numpy as jnp
from jax import lax
from jax.experimental import pallas as pl
from jax.experimental.pallas import tpu as pltpu
from jax.sharding import PartitionSpec as P

RECOVERY_STEPS = 4
PAIRS = ((0, 0), (0, 1), (0, 2), (1, 1), (1, 2), (2, 2))
FOUR_PI = 4.0 * math.pi
PACK = 87
PADX, PADY = 10, 12
NSEC = 4


def slot(i, j):
    return PAIRS.index((min(i, j), max(i, j)))


def row_of(t, xp, yp):
    return ((t * PADX + xp) * PADY + yp) * 8


def lanes():
    return lax.broadcasted_iota(jnp.int32, (8, 128), 1)


def rows_iota():
    return lax.broadcasted_iota(jnp.int32, (8, 128), 0)


def lroll(v, amount):
    amount = amount % 128
    return v if amount == 0 else pltpu.roll(v, amount, 1)


def shifted(f, halo, k, lane):
    if k > 0:
        return lroll(jnp.where(lane < k, halo, f), 128 - k)
    return lroll(jnp.where(lane >= 128 + k, halo, f), -k)


def d_one(m2, m1, p1, p2):
    return (8.0 / 12.0) * (p1 - m1) - (1.0 / 12.0) * (p2 - m2)


def line_derivs(v, second):
    s1 = v[1] + v[-1]
    s2 = v[2] + v[-2]
    s3 = v[3] + v[-3]
    first = (8.0 / 12.0) * (v[1] - v[-1]) - (1.0 / 12.0) * (v[2] - v[-2])
    kreiss = (0.2 / 64.0) * s3 - (0.2 * 6.0 / 64.0) * s2 + (0.2 * 15.0 / 64.0) * s1
    sec = None
    if second:
        sec = (16.0 / 12.0) * s1 - (1.0 / 12.0) * s2 - (30.0 / 12.0) * v[0]
    return first, kreiss, sec


def fanned(v, amount):
    if amount + 21 >= 128:
        v, amount = lroll(v, amount), 0
    return pltpu.roll(v, amount, 1, stride=3, stride_axis=0)


def expand(lo, hi, t, lane):
    up = fanned(hi, 128 - PACK + 24 * t)
    dn = fanned(lo, 125 - PACK + 24 * t)
    return jnp.where(lane < 3, up, dn)


def deriv_stage(T, G):
    lane = lanes()

    def tile(t, xp, yp):
        return T[pl.ds(pl.multiple_of(row_of(t, xp, yp), 8), 8), :]

    def packed(xp, yp):
        base = row_of(3, xp, yp)
        lo = jnp.broadcast_to(T[pl.ds(base + 6, 1), :], (8, 128))
        hi = jnp.broadcast_to(T[pl.ds(base + 7, 1), :], (8, 128))
        return lo, hi

    def body(xy, carry):
        x = xy // 4
        y = xy % 4
        xp, yp = x + 3, y + 4
        own_z = packed(xp, yp)
        zx = [packed(xp + a, yp) for a in (-2, -1, 1, 2)]
        zy = [packed(xp, yp + a) for a in (-2, -1, 1, 2)]
        dx_z = [d_one(*[zx[i][side] for i in range(4)]) for side in range(2)]
        dy_z = [d_one(*[zy[i][side] for i in range(4)]) for side in range(2)]

        def put(q, t, value):
            G[pl.ds(pl.multiple_of(((q * 3 + t - 1) * 16 + xy) * 8, 8), 8), :] = value

        for t in (1, 2, 3):
            second = t < 3
            vx = {a: tile(t, xp + a, yp) for a in range(-3, 4)}
            vy = {a: tile(t, xp, yp + a) if a else vx[0] for a in range(-3, 4)}
            halo = expand(own_z[0], own_z[1], t, lane)
            vz = {a: shifted(vx[0], halo, a, lane) if a else vx[0] for a in range(-3, 4)}
            dx, kx, sx = line_derivs(vx, second)
            dy, ky, sy = line_derivs(vy, second)
            dz, kz, sz = line_derivs(vz, second)
            put(0, t, dx)
            put(1, t, dy)
            put(2, t, dz)
            put(3, t, kx + ky + kz - (0.2 * 60.0 / 64.0) * vx[0])
            if second:
                rows = [
                    d_one(*[tile(t, xp + a, yp + b) for b in (-2, -1, 1, 2)])
                    for a in (-2, -1, 1, 2)
                ]
                put(4, t, sx)
                put(5, t, d_one(*rows))
                hx = expand(dx_z[0], dx_z[1], t, lane)
                hy = expand(dy_z[0], dy_z[1], t, lane)
                put(6, t, d_one(*[shifted(dx, hx, a, lane) for a in (-2, -1, 1, 2)]))
                put(7, t, sy)
                put(8, t, d_one(*[shifted(dy, hy, a, lane) for a in (-2, -1, 1, 2)]))
                put(9, t, sz)
        return carry

    lax.fori_loop(0, 16, body, 0)


def dot3(a, b):
    return a[0] * b[0] + a[1] * b[1] + a[2] * b[2]


def recover(cons, mag):
    density = cons[0]
    mom = cons[1:4]
    energy = cons[4] + density
    mom_sq = dot3(mom, mom)
    mag_sq = dot3(mag, mag)
    cross = dot3(mom, mag)
    cross_sq = cross * cross

    def state(z):
        zb = z + mag_sq
        zz = z * z
        speed_sq = (mom_sq * zz + cross_sq * (2.0 * z + mag_sq)) / (zz * zb * zb)
        ilsq = 1.0 - jnp.minimum(speed_sq, 0.99)
        rho = density * jnp.sqrt(ilsq)
        return ilsq, rho, 0.5 * (z * ilsq - rho)

    z = jnp.maximum(energy - 0.5 * mag_sq, density)
    for _ in range(RECOVERY_STEPS):
        ilsq, rho, p = state(z)
        res = z + mag_sq - p - 0.5 * mag_sq * ilsq - 0.5 * cross_sq / (z * z) - energy
        z = jnp.maximum(z - res / (1.0 - 0.5 * ilsq), density)
    ilsq, rho, p = state(z)
    p = jnp.maximum(p, 0.01 * rho)
    lor = 1.0 / jnp.sqrt(ilsq)
    factor = lor / (z + mag_sq)
    cz = cross / z
    return rho, p, [factor * (mom[i] + cz * mag[i]) for i in range(3)]


def prim_stage(T, PR, PH, EC, EH):
    lane = lanes()

    def strip(t, s, xp, dy=0):
        return T[pl.ds(row_of(t, xp + 1, 2 + dy) + s, 8, stride=8), :]

    def finish(cons, low, up, chi, lapse):
        root = chi * jnp.sqrt(chi)
        centred = [0.5 * (low[i] + up[i]) for i in range(3)]
        mag = [c * root for c in centred]
        rho, p, u = recover([c * root for c in cons], mag)
        inv = -lapse / jnp.sqrt(1.0 + dot3(u, u))
        vel = [a * inv for a in u]
        ele = [
            vel[(i + 1) % 3] * centred[(i + 2) % 3] - vel[(i + 2) % 3] * centred[(i + 1) % 3]
            for i in range(3)
        ]
        return [rho, p] + u + mag, ele

    def body(xp, carry):
        own = [strip(0, s, xp) for s in range(8)]
        zhi = strip(3, 7, xp)
        upper = [
            strip(0, 5, xp + 1),
            strip(0, 6, xp, 1),
            jnp.where(lane == 127, lroll(zhi, 127 - (PACK - 21)), lroll(own[7], 127)),
        ]
        prims, ele = finish(own[:5], own[5:], upper, strip(1, 0, xp), strip(1, 7, xp))
        at = pl.ds(pl.multiple_of(8 + xp * 8, 8), 8)
        for q in range(8):
            PR[q, at, :] = prims[q]
        for i in range(3):
            EC[i, at, :] = ele[i]
        return carry

    lax.fori_loop(0, 8, body, 0)

    def body_h(k, carry):
        xp = k + 1

        def halo(u, xq, dy=0):
            p = PACK - 3 * u
            return jnp.where(
                lane < 3, lroll(strip(3, 7, xq, dy), -p), lroll(strip(3, 6, xq, dy), 125 - p)
            )

        vals = [halo(u, xp) for u in range(9)]
        first = T[pl.ds(row_of(0, xp + 1, 2) + 7, 8, stride=8), :]
        upper = [
            halo(5, xp + 1),
            halo(6, xp, 1),
            lroll(jnp.where(lane == 0, first, vals[7]), 127),
        ]
        prims, ele = finish(vals[:5], vals[5:8], upper, vals[8], halo(15, xp))
        at = pl.ds(pl.multiple_of(8 + k * 8, 8), 8)
        for q in range(8):
            PH[q, at, :] = prims[q]
        for i in range(3):
            EH[i, at, :] = ele[i]
        return carry

    lax.fori_loop(0, 6, body_h, 0)


def limited(a, b):
    return jnp.maximum(jnp.minimum(a, b), 0.0) + jnp.minimum(jnp.maximum(a, b), 0.0)


def stress_parts(rho, p, u, mag):
    lor_sq = 1.0 + dot3(u, u)
    lor = jnp.sqrt(lor_sq)
    inv = 1.0 / lor
    vel = [a * inv for a in u]
    along = dot3(vel, mag)
    b0 = lor * along
    b = [mag[i] * inv + b0 * vel[i] for i in range(3)]
    bsq = dot3(mag, mag) * (inv * inv) + along * along
    enth = rho + 2.0 * p
    inertia = enth + bsq
    return lor, lor_sq, vel, b0, b, bsq, enth, inertia, p + 0.5 * bsq


def face_state(rho, p, u, mag, d):
    lor, lor_sq, vel, b0, b, bsq, enth, inertia, ptot = stress_parts(rho, p, u, mag)
    dens = rho * lor
    wl = inertia * lor_sq
    mom = [wl * vel[j] - b0 * b[j] for j in range(3)]
    cons = [dens] + mom + [wl - ptot - b0 * b0 - dens]
    wv = wl * vel[d]
    flux = [dens * vel[d]]
    for j in range(3):
        f = wv * vel[j] - b[d] * b[j]
        flux.append(f + ptot if j == d else f)
    flux.append(mom[d] - dens * vel[d])
    vsq = dot3(vel, vel)
    cs = 2.0 * p / enth
    va = bsq / inertia
    a2 = cs + va - cs * va
    vd = vel[d]
    spread = jnp.sqrt(a2 * (1.0 - vsq) * (1.0 - vsq * a2 - vd * vd * (1.0 - a2)))
    mid = vd * (1.0 - a2)
    fast = jnp.maximum(jnp.abs(mid + spread), jnp.abs(mid - spread)) / (1.0 - vsq * a2)
    return cons, flux, fast


def face_flux(left, right, normal, chi, lapse, d):
    root = chi * jnp.sqrt(chi)
    states = []
    for side in (left, right):
        mag = list(side[5:8])
        mag[d] = normal * root
        states.append(face_state(side[0], side[1], side[2:5], mag, d))
    (cl, fl, sl), (cr, fr, sr) = states
    sig = jnp.maximum(sl, sr)
    weight = 0.5 * lapse / root
    return [weight * (fl[q] + fr[q] - sig * (cr[q] - cl[q])) for q in range(5)]


def recon(m2, m1, c0, p1):
    mid = c0 - m1
    return m1 + 0.5 * limited(m1 - m2, mid), c0 - 0.5 * limited(mid, p1 - c0)


def flux_stage(T, PR, PH, FX, HR):
    lane = lanes()

    def strip(t, s, x, dy=0):
        return T[pl.ds(row_of(t, x + 3, 2 + dy) + s, 8, stride=8), :]

    def prim(q, x, dy=0):
        return PR[q, pl.ds(8 + (x + 2) * 8 + dy, 8), :]

    def half(a, b):
        return 0.5 * (a + b)

    def body_x(i, carry):
        both = [recon(*[prim(q, i + a) for a in (-2, -1, 0, 1)]) for q in range(8)]
        chi = half(strip(1, 0, i - 1), strip(1, 0, i))
        lapse = half(strip(1, 7, i - 1), strip(1, 7, i))
        out = face_flux([b[0] for b in both], [b[1] for b in both], strip(0, 5, i), chi, lapse, 0)
        at = pl.ds(pl.multiple_of(i * 8, 8), 8)
        for q in range(5):
            FX[q, at, :] = out[q]
        return carry

    lax.fori_loop(0, 5, body_x, 0)

    def body(x, carry):
        at = pl.ds(pl.multiple_of(x * 8, 8), 8)
        up = pl.ds(pl.multiple_of(x * 8 + 8, 8), 8)
        chi0, lapse0 = strip(1, 0, x), strip(1, 7, x)
        both = [recon(*[prim(q, x, a) for a in (-2, -1, 0, 1)]) for q in range(8)]
        chi = half(strip(1, 0, x, -1), chi0)
        lapse = half(strip(1, 7, x, -1), lapse0)
        fy = face_flux([b[0] for b in both], [b[1] for b in both], strip(0, 6, x), chi, lapse, 1)
        zlo, zhi = strip(3, 6, x), strip(3, 7, x)

        def halo(u):
            p = PACK - 3 * u
            return jnp.where(lane < 3, lroll(zhi, -p), lroll(zlo, 125 - p))

        chih, lapseh = halo(8), halo(15)
        own = [prim(q, x) for q in range(8)]
        hal = [PH[q, pl.ds(pl.multiple_of(8 + (x + 1) * 8, 8), 8), :] for q in range(8)]
        both = [
            recon(
                shifted(own[q], hal[q], -2, lane),
                shifted(own[q], hal[q], -1, lane),
                own[q],
                shifted(own[q], hal[q], 1, lane),
            )
            for q in range(8)
        ]
        bz = strip(0, 7, x)
        fz = face_flux(
            [b[0] for b in both],
            [b[1] for b in both],
            bz,
            half(shifted(chi0, chih, -1, lane), chi0),
            half(shifted(lapse0, lapseh, -1, lane), lapse0),
            2,
        )
        both = [
            recon(lroll(own[q], 2), lroll(own[q], 1), hal[q], lroll(hal[q], 127)) for q in range(8)
        ]
        fl = face_flux(
            [b[0] for b in both],
            [b[1] for b in both],
            halo(7),
            half(lroll(chi0, 1), chih),
            half(lroll(lapse0, 1), lapseh),
            2,
        )
        for q in range(5):
            FX[5 + q, at, :] = fy[q]
        for q in range(5):
            fzu = lroll(jnp.where(lane == 0, fl[q], fz[q]), 127)
            fyu = FX[5 + q, pl.ds(x * 8 + 1, 8), :]
            HR[q, at, :] = (fz[q] - fzu) + (fy[q] - fyu) + (FX[q, at, :] - FX[q, up, :])
        return carry

    lax.fori_loop(0, 4, body, 0)


def field_stage(EC, EH, EZ, HR):
    lane = lanes()

    def ec(i, x, dy=0):
        return EC[i, pl.ds(8 + (x + 2) * 8 + dy, 8), :]

    def eh(i, x, dy=0):
        return EH[i, pl.ds(8 + (x + 1) * 8 + dy, 8), :]

    for x in range(5):
        at = pl.ds(x * 8, 8)
        EZ[0, at, :] = 0.25 * (ec(2, x - 1, -1) + ec(2, x, -1) + ec(2, x - 1) + ec(2, x))
        s = ec(1, x - 1) + ec(1, x)
        h = eh(1, x - 1) + eh(1, x)
        EZ[1, at, :] = 0.25 * (shifted(s, h, -1, lane) + s)
        EZ[2, at, :] = 0.25 * (shifted(s, h, 1, lane) + s)
        if x < 4:
            s = ec(0, x, -1) + ec(0, x)
            h = eh(0, x, -1) + eh(0, x)
            EZ[3, at, :] = 0.25 * (shifted(s, h, -1, lane) + s)
            EZ[4, at, :] = 0.25 * (shifted(s, h, 1, lane) + s)
    for x in range(4):
        at, up, yu = pl.ds(x * 8, 8), pl.ds(x * 8 + 8, 8), pl.ds(x * 8 + 1, 8)
        ez = EZ[0, at, :]
        HR[5, at, :] = (EZ[2, at, :] - EZ[1, at, :]) - (EZ[0, yu, :] - ez)
        HR[6, at, :] = (EZ[0, up, :] - ez) - (EZ[4, at, :] - EZ[3, at, :])
        HR[7, at, :] = (EZ[3, yu, :] - EZ[3, at, :]) - (EZ[1, up, :] - EZ[1, at, :])


def sym(values):
    return [[values[slot(i, j)] for j in range(3)] for i in range(3)]


def trace(inv, m):
    return (
        inv[0][0] * m[0][0]
        + inv[1][1] * m[1][1]
        + inv[2][2] * m[2][2]
        + 2.0 * (inv[0][1] * m[0][1] + inv[0][2] * m[0][2] + inv[1][2] * m[1][2])
    )


def inverse(g):
    c00 = g[1][1] * g[2][2] - g[1][2] * g[1][2]
    c01 = g[0][2] * g[1][2] - g[0][1] * g[2][2]
    c02 = g[0][1] * g[1][2] - g[0][2] * g[1][1]
    c11 = g[0][0] * g[2][2] - g[0][2] * g[0][2]
    c12 = g[0][1] * g[0][2] - g[0][0] * g[1][2]
    c22 = g[0][0] * g[1][1] - g[0][1] * g[0][1]
    r = 1.0 / (g[0][0] * c00 + g[0][1] * c01 + g[0][2] * c02)
    return sym([c00 * r, c01 * r, c02 * r, c11 * r, c12 * r, c22 * r])


R3 = range(3)


def algebra_stage(G, PR, HR, o_st, o_fl, RT):
    low = rows_iota() < 4

    def body(h, carry):
        x = 2 * h

        def fold(a, b):
            return jnp.where(low, a, b)

        at = pl.ds(pl.multiple_of(8 * h, 8), 8)

        def strip(ref, q, pad):
            return fold(
                ref[q, pl.ds(pad + x * 8 + 2, 8), :], ref[q, pl.ds(pad + x * 8 + 8 - 2, 8), :]
            )

        def g(q, v):
            return G[pl.ds(((q * 3 + v // 8) * 16 + 8 * h) * 8 + v % 8, 8, stride=8), :]

        cur = [o_st[v, at, :] for v in range(22)]
        flu = [o_fl[v, at, :] for v in range(8)]
        prims = [strip(PR, q, 8 + 16) for q in range(8)]

        def grad(v):
            return [g(k, v) for k in R3]

        def hess(v):
            return sym([g(4 + s, v) for s in range(6)])

        chi, lapse = cur[0], cur[7]
        metric = sym(cur[1:7])
        shift = cur[8:11]
        khat, theta = cur[11], cur[21]
        trl = sym(cur[12:18])
        conn = cur[18:21]
        inv = inverse(metric)
        ichi = 1.0 / chi
        root = chi * jnp.sqrt(chi)
        ktot = khat + 2.0 * theta

        lor, lor_sq, vel, b0, b, bsq, enth, inertia, ptot = stress_parts(
            prims[0], prims[1], prims[2:5], prims[5:8]
        )
        wl = inertia * lor_sq
        stress = sym(
            [
                wl * vel[i] * vel[j] - b[i] * b[j] + (ptot if i == j else 0.0)
                for i, j in PAIRS
            ]
        )
        total = flu[4] + flu[0]
        dens = total * root
        mom = [flu[1 + i] * root for i in R3]
        dal = grad(7)
        dsh = [grad(8 + i) for i in R3]
        hydro = [strip(HR, q, 0) for q in range(8)]
        for i in R3:
            hydro[1 + i] = (
                hydro[1 + i]
                - total * dal[i]
                + (flu[1] * dsh[0][i] + flu[2] * dsh[1][i] + flu[3] * dsh[2][i])
            )
        third = ktot * (1.0 / 3.0)
        curv = sym([(trl[i][j] + metric[i][j] * third) * ichi for i, j in PAIRS])
        tk = (
            stress[0][0] * curv[0][0]
            + stress[1][1] * curv[1][1]
            + stress[2][2] * curv[2][2]
            + 2.0
            * (stress[0][1] * curv[0][1] + stress[0][2] * curv[0][2] + stress[1][2] * curv[1][2])
        )
        hydro[4] = hydro[4] + lapse / root * tk - dot3(flu[1:4], dal)
        for q in range(8):
            RT[22 + q, at, :] = hydro[q]

        def adv(gr):
            return shift[0] * gr[0] + shift[1] * gr[1] + shift[2] * gr[2]

        def emit(v, rate):
            RT[v, at, :] = rate + g(3, v)

        dg = [[grad(1 + slot(i, j)) if i <= j else None for j in R3] for i in R3]
        dg = [[dg[min(i, j)][max(i, j)] for j in R3] for i in R3]
        lowered = [
            sym([0.5 * (dg[i][k][j] + dg[i][j][k] - dg[j][k][i]) for j, k in PAIRS]) for i in R3
        ]
        raised = [
            sym(
                [
                    inv[i][0] * lowered[0][j][k]
                    + inv[i][1] * lowered[1][j][k]
                    + inv[i][2] * lowered[2][j][k]
                    for j, k in PAIRS
                ]
            )
            for i in R3
        ]
        gd = [trace(inv, raised[i]) for i in R3]
        dchi = grad(0)
        hchi = hess(0)
        xcov = sym(
            [hchi[i][j] - dot3([raised[k][i][j] for k in R3], dchi) for i, j in PAIRS]
        )
        chi_lap = trace(inv, xcov)
        uchi = [dot3(inv[i], dchi) for i in R3]
        chi_sq = dot3(uchi, dchi)
        cross = dot3(uchi, dal)
        hal = hess(7)
        half_ichi = 0.5 * ichi
        lcov = sym(
            [
                hal[i][j]
                - dot3([raised[k][i][j] for k in R3], dal)
                + (dchi[i] * dal[j] + dchi[j] * dal[i] - metric[i][j] * cross) * half_ichi
                for i, j in PAIRS
            ]
        )
        lapse_lap = chi * trace(inv, lcov)
        dgam = [grad(18 + i) for i in R3]
        cu = [
            [
                [
                    inv[l][0] * lowered[j][k][0]
                    + inv[l][1] * lowered[j][k][1]
                    + inv[l][2] * lowered[j][k][2]
                    for l in R3
                ]
                for k in R3
            ]
            for j in R3
        ]
        quarter = half_ichi * half_ichi
        ricci = []
        for i, j in PAIRS:
            v = 1 + slot(i, j)
            hg = hess(v)
            r = -0.5 * trace(inv, hg)
            for k in R3:
                r = r + 0.5 * (metric[k][i] * dgam[k][j] + metric[k][j] * dgam[k][i])
                r = r + 0.5 * gd[k] * (lowered[i][j][k] + lowered[j][i][k])
            for k in R3:
                for l in R3:
                    r = r + raised[k][l][i] * cu[j][k][l]
                    r = r + raised[k][l][j] * cu[i][k][l]
                    r = r + raised[k][i][l] * cu[k][j][l]
            r = r + (xcov[i][j] + metric[i][j] * chi_lap) * half_ichi
            r = r - (dchi[i] * dchi[j] + 3.0 * metric[i][j] * chi_sq) * quarter
            ricci.append(r)
        ricci = sym(ricci)
        rscal = chi * trace(inv, ricci)
        strace = chi * trace(inv, stress)
        mixed = [[dot3(inv[i], [trl[k][j] for k in R3]) for j in R3] for i in R3]
        up = sym([dot3(mixed[i], inv[j]) for i, j in PAIRS])
        aa = trace(trl, up)
        div = dsh[0][0] + dsh[1][1] + dsh[2][2]
        div23 = (2.0 / 3.0) * div

        emit(0, adv(dchi) + (2.0 / 3.0) * chi * (lapse * ktot - div))
        emit(7, adv(dal) - 2.0 * lapse * khat)
        for i in R3:
            emit(8 + i, adv(dsh[i]) + 0.75 * conn[i] - shift[i])
        dkh = grad(11)
        dth = grad(21)
        emit(
            11,
            adv(dkh)
            - lapse_lap
            + lapse * (aa + ktot * third)
            + FOUR_PI * lapse * (strace + dens)
            + 0.02 * lapse * theta,
        )
        src = sym(
            [
                -lcov[i][j] + lapse * (ricci[i][j] - (2.0 * FOUR_PI) * stress[i][j])
                for i, j in PAIRS
            ]
        )
        strc = trace(inv, src) * (1.0 / 3.0)
        for i, j in PAIRS:
            s = slot(i, j)
            acc = adv(dg[i][j])
            for k in R3:
                acc = acc + metric[i][k] * dsh[k][j] + metric[j][k] * dsh[k][i]
            emit(1 + s, acc - metric[i][j] * div23 - 2.0 * lapse * trl[i][j])
            prod = dot3(trl[i], [mixed[k][j] for k in R3])
            acc = adv(grad(12 + s))
            for k in R3:
                acc = acc + trl[i][k] * dsh[k][j] + trl[j][k] * dsh[k][i]
            emit(
                12 + s,
                acc
                - trl[i][j] * div23
                + chi * (src[i][j] - metric[i][j] * strc)
                + lapse * (ktot * trl[i][j] - 2.0 * prod),
            )
        hsh = [hess(8 + i) for i in R3]
        ddiv = [hsh[0][0][j] + hsh[1][1][j] + hsh[2][2][j] for j in R3]
        for i in R3:
            br = trace(up, raised[i])
            br = br - 1.5 * ichi * dot3(up[i], dchi)
            br = br - (1.0 / 3.0) * dot3(inv[i], [2.0 * dkh[j] + dth[j] for j in R3])
            br = br - (2.0 * FOUR_PI) * dot3(inv[i], mom)
            emit(
                18 + i,
                adv(dgam[i])
                - dot3(gd, dsh[i])
                + gd[i] * div23
                + trace(inv, hsh[i])
                + (1.0 / 3.0) * dot3(inv[i], ddiv)
                - 2.0 * dot3(up[i], dal)
                + 2.0 * lapse * br
                - 0.04 * lapse * (conn[i] - gd[i]),
            )
        emit(
            21,
            adv(dth)
            + 0.5
            * lapse
            * (rscal - aa + (2.0 / 3.0) * ktot * ktot - (4.0 * FOUR_PI) * dens)
            - 0.04 * lapse * theta,
        )
        return carry

    lax.fori_loop(0, 2, body, 0)


def compute_scratch():
    V = lambda *s: pltpu.VMEM(s, jnp.float32)
    return [
        V(10 * 3 * 16 * 8, 128),
        V(8, 80, 128),
        V(8, 64, 128),
        V(3, 80, 128),
        V(3, 64, 128),
        V(10, 48, 128),
        V(8, 48, 128),
        V(5, 48, 128),
    ]


def rates(T, scratch, o_st, o_fl, RT):
    G, PR, PH, EC, EH, FX, HR, EZ = scratch
    prim_stage(T, PR, PH, EC, EH)
    flux_stage(T, PR, PH, FX, HR)
    field_stage(EC, EH, EZ, HR)
    deriv_stage(T, G)
    algebra_stage(G, PR, HR, o_st, o_fl, RT)


MESH = pl.DeviceIdType.MESH
N_SLOTS = 29


def wave_stage(own):
    metric = sym([own(8 + v) for v in range(1, 7)])
    inv = inverse(metric)
    scale = 2.0 * own(8 + 7) * own(8)
    speeds = [jnp.abs(own(16 + d)) + jnp.sqrt(scale * inv[d][d]) for d in range(3)]
    return jnp.maximum(jnp.maximum(speeds[0], speeds[1]), speeds[2])


def load_stage(st, fl, o_st, o_fl, T):
    for u in range(30):
        src, dst, v = (fl, o_fl, u) if u < 8 else (st, o_st, u - 8)
        for x in range(4):
            value = src[v, x]
            T[pl.ds(row_of(u // 8, x + 3, 4) + u % 8, 4, stride=8), :] = value
            dst[v, pl.ds(4 * x, 4), :] = value


def local_stage(o_st, o_fl, zsend, mine):
    lane = lanes()

    def body(h, top):
        at = pl.ds(pl.multiple_of(8 * h, 8), 8)

        def own(u):
            return o_fl[u, at, :] if u < 8 else o_st[u - 8, at, :]

        last = jnp.zeros((8, 128), jnp.float32)
        first = jnp.zeros((8, 128), jnp.float32)
        for u in range(30):
            p = PACK - 3 * u
            here = (lane >= p) & (lane < p + 3)
            value = own(u)
            first = jnp.where(here, lroll(value, p), first)
            last = jnp.where(here, lroll(value, p - 125), last)
        zsend[0, at, :] = last
        zsend[1, at, :] = first
        return jnp.maximum(top, wave_stage(own))

    top = lax.fori_loop(0, 2, body, jnp.zeros((8, 128), jnp.float32))
    mine[0] = jnp.max(top, axis=0, keepdims=True)


def halo_rows(zrecv, T):
    for side in range(2):
        for x in range(4):
            T[pl.ds(row_of(3, x + 3, 4) + 6 + side, 4, stride=8), :] = zrecv[
                side, pl.ds(4 * x, 4), :
            ]


def kernel(st, fl, o_st, o_fl, T5, zsend, zrecv, mine, slots, RT, ssem, rsem, msem, *scratch):
    gx, gy, gz = lax.axis_index("gx"), lax.axis_index("gy"), lax.axis_index("gz")
    hi = gy % 2
    T = T5.reshape(3840, 128)

    def at_x(step):
        x2 = (hi * 4 + gz + step) % 8
        return (gx, gy - hi + x2 // 4, x2 % 4)

    ring_x = [at_x(k) for k in range(1, 8)]
    ring_y = [(gx, (gy + 2 * k) % 16, gz) for k in range(1, 8)]
    ring_z = [((gx + k) % 16, gy, gz) for k in range(1, 16)]
    x_up, x_dn = ((gx + 1) % 16, gy, gz), ((gx + 15) % 16, gy, gz)
    z_up, z_dn = (gx, gy, (gz + 1) % 4), (gx, gy, (gz + 3) % 4)
    partner = at_x(4)
    onward = (gx, (gy + 2 - 4 * hi + 16) % 16, gz)

    barrier = pltpu.get_barrier_semaphore()
    for peer in ring_x + ring_y + ring_z:
        pl.semaphore_signal(barrier, inc=1, device_id=peer, device_id_type=MESH)
    load_stage(st, fl, o_st, o_fl, T)
    local_stage(o_st, o_fl, zsend, mine)
    pl.semaphore_wait(barrier, N_SLOTS)

    started = []

    def send(src, dst, peer):
        k = len(started)
        copy = pltpu.make_async_remote_copy(
            src_ref=src,
            dst_ref=dst,
            send_sem=ssem.at[k],
            recv_sem=rsem.at[k],
            device_id=peer,
            device_id_type=MESH,
        )
        copy.start()
        started.append(copy)
        return copy

    def share(phase, base, peers):
        for k, peer in enumerate(peers):
            pltpu.make_async_remote_copy(
                src_ref=mine.at[phase],
                dst_ref=slots.at[base + k],
                send_sem=msem.at[phase],
                recv_sem=msem.at[3 + phase],
                device_id=peer,
                device_id_type=MESH,
            ).start()

    def gathered(phase, base, count):
        part = slots.at[pl.ds(base, count)]
        pltpu.make_async_copy(part, part, msem.at[3 + phase]).wait()
        mine[phase + 1] = jnp.maximum(mine[phase], jnp.max(slots[pl.ds(base, count)], axis=0))

    def drained(phase, base, count):
        part = slots.at[pl.ds(base, count)]
        pltpu.make_async_copy(part, part, msem.at[phase]).wait()

    def block(t, n, xp, nx, yp, ny):
        return T5.at[pl.ds(t, n), pl.ds(xp, nx), pl.ds(yp, ny)]

    def to_partner(t):
        return send(block(t, 1, 3, 4, 4, 4), block(t, 1, 3, 4, 8 * hi, 4), partner)

    def go_on(t):
        return send(block(t, 1, 3, 4, 9 - 9 * hi, 3), block(t, 1, 3, 4, 1 + 7 * hi, 3), onward)

    def faces(t, n):
        return [
            send(block(t, n, 3, 3, 4, 4), block(t, n, 7, 3, 4, 4), x_dn),
            send(block(t, n, 4, 3, 4, 4), block(t, n, 0, 3, 4, 4), x_up),
        ]

    def edges(t, n):
        copies = []
        for yp in (2, 8):
            copies.append(send(block(t, n, 3, 2, yp, 2), block(t, n, 7, 2, yp, 2), x_dn))
            copies.append(send(block(t, n, 5, 2, yp, 2), block(t, n, 1, 2, yp, 2), x_up))
        return copies

    zs = [send(zsend.at[0], zrecv.at[0], z_up), send(zsend.at[1], zrecv.at[1], z_dn)]
    share(0, 0, ring_x)
    far = [to_partner(t) for t in range(3)]
    side = faces(0, 3)
    for copy in zs:
        copy.wait_recv()
    halo_rows(zrecv, T)
    far.append(to_partner(3))
    side += faces(3, 1)
    gathered(0, 0, 7)
    share(1, 7, ring_y)
    relay = []
    for t in range(2):
        far[t].wait_recv()
        relay.append(go_on(t))
    gathered(1, 7, 7)
    share(2, 14, ring_z)
    for t in range(2, 4):
        far[t].wait_recv()
        relay.append(go_on(t))
    for t in range(2):
        relay[t].wait_recv()
    side += edges(0, 2)
    for t in range(2, 4):
        relay[t].wait_recv()
    side += edges(2, 2)
    for copy in side:
        copy.wait_recv()

    rates(T, scratch, o_st, o_fl, RT)
    gathered(2, 14, 15)
    step = 0.25 / jnp.max(mine[3], axis=1, keepdims=True)
    for v in range(22):
        o_st[v] = o_st[v] + step * RT[v]
    for v in range(8):
        o_fl[v] = o_fl[v] + step * RT[22 + v]
    for copy in started:
        copy.wait_send()
    drained(0, 0, 7)
    drained(1, 7, 7)
    drained(2, 14, 15)


N_COPIES = 2 + 8 + 4 + 8


def per_device(spacetime, fluid):
    vmem = pl.BlockSpec(memory_space=pltpu.VMEM)
    space = lambda *s: pltpu.VMEM(s, jnp.float32)
    st_new, fl_new = pl.pallas_call(
        kernel,
        out_shape=(
            jax.ShapeDtypeStruct((22, 16, 128), jnp.float32),
            jax.ShapeDtypeStruct((8, 16, 128), jnp.float32),
        ),
        in_specs=[vmem, vmem],
        out_specs=(vmem, vmem),
        scratch_shapes=[
            space(4, PADX, PADY, 8, 128),
            space(2, 16, 128),
            space(2, 16, 128),
            space(4, 1, 128),
            space(N_SLOTS, 1, 128),
            space(30, 16, 128),
            pltpu.SemaphoreType.DMA((30,)),
            pltpu.SemaphoreType.DMA((30,)),
            pltpu.SemaphoreType.DMA((6,)),
        ]
        + compute_scratch(),
        compiler_params=pltpu.CompilerParams(collective_id=1, has_side_effects=True),
    )(spacetime, fluid)
    return st_new.reshape(22, 4, 4, 128), fl_new.reshape(8, 4, 4, 128)


def solution(mesh):
    spec = P(None, "gx", "gy", "gz")
    return jax.shard_map(
        per_device, mesh=mesh, in_specs=(spec, spec), out_specs=(spec, spec), check_vma=False
    )
```

time: 239 us -> 58.8 us (0.25)
  the two profiles are of different devices: /device:TPU:1 before, /device:TPU:3 now
where the time goes in v1:
time: 58.8 us; the launch traced here: 58.6 us
  Pallas kernels  55.7 us (95%)
  local copies, waits for them, and re-layouts  2.27 us (4%)
  between operations  0.65 us (1%)
    pallas_call x1, Pallas kernels, per_device(): pl.pallas_call(kernel, out_shape=(jax.ShapeDtypeStruct((22, 16, 128), jnp...  55.7 us
    unnamed x4, local copies, waits for them, and re-layouts  2.27 us

profile of v1, /device:TPU:3, one launch (start us, length us, event | category | flops | bytes accessed | tf_op | source)
XLA Modules:
  0.0 58.6 jit_solution(4914330739008839696)
XLA Ops:
  0.6 55.7 %shard_map.41 = (f32[22,16,128]{2,1,0:T(8,128)}, f32[8,16,128]{2,1,0:T(8,128)}) custom-call(f32[22,4,4,128]{3,2,1,0:T(4,128)} %st.1, f32[8,4,4,128]{3,2,1,0:T(4,128)} %fl.1), custom_call_target="tpu_custom_call" | custom-call | tf_op jit(solution)/shard_map/pallas_call | solution.py:856
  56.3 0.0 copy-start
  56.3 1.6 %copy.6 = f32[22,4,4,128]{3,2,1,0:T(4,128)} copy(f32[22,4,4,128]{3,2,1,0:T(4,128)} %bitcast.2) | data formatting | bytes 360448
  58.0 0.0 copy-done
  58.0 0.6 %copy.7 = f32[8,4,4,128]{3,2,1,0:T(4,128)} copy(f32[8,4,4,128]{3,2,1,0:T(4,128)S(1)} %bitcast.3) | data formatting | bytes 131072
Async XLA Ops:
  56.3 1.6 %copy-start = (f32[8,16,128]{2,1,0:T(8,128)S(1)}, f32[8,16,128]{2,1,0:T(8,128)}, u32[]{:S(2)}) copy-start(f32[8,16,128]{2,1,0:T(8,128)} %get-tuple-element.5) | copy-start | bytes 196612

commit v2 on v1

--- a/solution.py
+++ b/solution.py
@@ -9,13 +9,23 @@
 RECOVERY_STEPS = 4
 PAIRS = ((0, 0), (0, 1), (0, 2), (1, 1), (1, 2), (2, 2))
 FOUR_PI = 4.0 * math.pi
-PACK = 87
+PACK = 93
+Z_TILE = 2
 PADX, PADY = 10, 12
-NSEC = 4
+PLACE = (
+    [(1, s) for s in range(8)]
+    + [(2, 0), (2, 1), (2, 2)]
+    + [(3, s) for s in range(7)]
+    + [(2, 3), (2, 4), (2, 5), (3, 7)]
+)
 
 
 def slot(i, j):
     return PAIRS.index((min(i, j), max(i, j)))
+
+
+def aligned(start):
+    return pl.ds(start if isinstance(start, int) else pl.multiple_of(start, 8), 8)
 
 
 def row_of(t, xp, yp):
@@ -69,60 +79,87 @@
     return jnp.where(lane < 3, up, dn)
 
 
-def deriv_stage(T, G):
+def tile_at(T, t, xp, yp):
+    return T[aligned(row_of(t, xp, yp)), :]
+
+
+def packed_at(T, xp, yp):
+    base = row_of(Z_TILE, xp, yp)
+    return [jnp.broadcast_to(T[pl.ds(base + 6 + side, 1), :], (8, 128)) for side in range(2)]
+
+
+def deriv_at(q, t, xy):
+    return aligned(((q * 3 + t - 1) * 16 + xy) * 8)
+
+
+NEAR = (-2, -1, 1, 2)
+
+
+def by_four(column):
+    def body(x, carry):
+        for y in range(4):
+            column(4 * x + y)
+        return carry
+
+    lax.fori_loop(0, 4, body, 0)
+
+
+def deriv_xz(T, G, tiles):
     lane = lanes()
 
-    def tile(t, xp, yp):
-        return T[pl.ds(pl.multiple_of(row_of(t, xp, yp), 8), 8), :]
-
-    def packed(xp, yp):
-        base = row_of(3, xp, yp)
-        lo = jnp.broadcast_to(T[pl.ds(base + 6, 1), :], (8, 128))
-        hi = jnp.broadcast_to(T[pl.ds(base + 7, 1), :], (8, 128))
-        return lo, hi
-
-    def body(xy, carry):
-        x = xy // 4
-        y = xy % 4
-        xp, yp = x + 3, y + 4
-        own_z = packed(xp, yp)
-        zx = [packed(xp + a, yp) for a in (-2, -1, 1, 2)]
-        zy = [packed(xp, yp + a) for a in (-2, -1, 1, 2)]
-        dx_z = [d_one(*[zx[i][side] for i in range(4)]) for side in range(2)]
-        dy_z = [d_one(*[zy[i][side] for i in range(4)]) for side in range(2)]
-
-        def put(q, t, value):
-            G[pl.ds(pl.multiple_of(((q * 3 + t - 1) * 16 + xy) * 8, 8), 8), :] = value
-
-        for t in (1, 2, 3):
+    def column(xy):
+        xp, yp = xy // 4 + 3, xy % 4 + 4
+        own = packed_at(T, xp, yp)
+        around = [packed_at(T, xp + a, yp) for a in NEAR]
+        border = [d_one(*[around[i][side] for i in range(4)]) for side in range(2)]
+        for t in tiles:
             second = t < 3
-            vx = {a: tile(t, xp + a, yp) for a in range(-3, 4)}
-            vy = {a: tile(t, xp, yp + a) if a else vx[0] for a in range(-3, 4)}
-            halo = expand(own_z[0], own_z[1], t, lane)
+            vx = {a: tile_at(T, t, xp + a, yp) for a in range(-3, 4)}
+            halo = expand(own[0], own[1], t, lane)
             vz = {a: shifted(vx[0], halo, a, lane) if a else vx[0] for a in range(-3, 4)}
             dx, kx, sx = line_derivs(vx, second)
+            dz, kz, sz = line_derivs(vz, second)
+            G[deriv_at(0, t, xy), :] = dx
+            G[deriv_at(2, t, xy), :] = dz
+            G[deriv_at(3, t, xy), :] = kx + kz - (0.2 * 60.0 / 64.0) * vx[0]
+            if second:
+                cross = expand(border[0], border[1], t, lane)
+                G[deriv_at(4, t, xy), :] = sx
+                G[deriv_at(6, t, xy), :] = d_one(*[shifted(dx, cross, a, lane) for a in NEAR])
+                G[deriv_at(9, t, xy), :] = sz
+
+    by_four(column)
+
+
+def deriv_y(T, G, tiles):
+    lane = lanes()
+
+    def column(xy):
+        xp, yp = xy // 4 + 3, xy % 4 + 4
+        around = [packed_at(T, xp, yp + a) for a in NEAR]
+        border = [d_one(*[around[i][side] for i in range(4)]) for side in range(2)]
+        for t in tiles:
+            second = t < 3
+            vy = {a: tile_at(T, t, xp, yp + a) for a in range(-3, 4)}
             dy, ky, sy = line_derivs(vy, second)
-            dz, kz, sz = line_derivs(vz, second)
-            put(0, t, dx)
-            put(1, t, dy)
-            put(2, t, dz)
-            put(3, t, kx + ky + kz - (0.2 * 60.0 / 64.0) * vx[0])
+            G[deriv_at(1, t, xy), :] = dy
+            G[deriv_at(3, t, xy), :] = G[deriv_at(3, t, xy), :] + ky
             if second:
-                rows = [
-                    d_one(*[tile(t, xp + a, yp + b) for b in (-2, -1, 1, 2)])
-                    for a in (-2, -1, 1, 2)
-                ]
-                put(4, t, sx)
-                put(5, t, d_one(*rows))
-                hx = expand(dx_z[0], dx_z[1], t, lane)
-                hy = expand(dy_z[0], dy_z[1], t, lane)
-                put(6, t, d_one(*[shifted(dx, hx, a, lane) for a in (-2, -1, 1, 2)]))
-                put(7, t, sy)
-                put(8, t, d_one(*[shifted(dy, hy, a, lane) for a in (-2, -1, 1, 2)]))
-                put(9, t, sz)
-        return carry
-
-    lax.fori_loop(0, 16, body, 0)
+                cross = expand(border[0], border[1], t, lane)
+                G[deriv_at(7, t, xy), :] = sy
+                G[deriv_at(8, t, xy), :] = d_one(*[shifted(dy, cross, a, lane) for a in NEAR])
+
+    by_four(column)
+
+
+def deriv_xy(T, G, tiles):
+    def column(xy):
+        xp, yp = xy // 4 + 3, xy % 4 + 4
+        for t in tiles:
+            rows = [d_one(*[tile_at(T, t, xp + a, yp + b) for b in NEAR]) for a in NEAR]
+            G[deriv_at(5, t, xy), :] = d_one(*rows)
+
+    by_four(column)
 
 
 def dot3(a, b):
@@ -159,7 +196,7 @@
     return rho, p, [factor * (mom[i] + cz * mag[i]) for i in range(3)]
 
 
-def prim_stage(T, PR, PH, EC, EH):
+def prim_stage(T, PR, PH, EC, EH, columns, halo_columns):
     lane = lanes()
 
     def strip(t, s, xp, dy=0):
@@ -178,49 +215,49 @@
         ]
         return [rho, p] + u + mag, ele
 
-    def body(xp, carry):
+    def body(xp):
         own = [strip(0, s, xp) for s in range(8)]
-        zhi = strip(3, 7, xp)
+        zhi = strip(Z_TILE, 7, xp)
         upper = [
             strip(0, 5, xp + 1),
             strip(0, 6, xp, 1),
             jnp.where(lane == 127, lroll(zhi, 127 - (PACK - 21)), lroll(own[7], 127)),
         ]
         prims, ele = finish(own[:5], own[5:], upper, strip(1, 0, xp), strip(1, 7, xp))
-        at = pl.ds(pl.multiple_of(8 + xp * 8, 8), 8)
+        at = aligned(8 + xp * 8)
         for q in range(8):
             PR[q, at, :] = prims[q]
         for i in range(3):
             EC[i, at, :] = ele[i]
-        return carry
-
-    lax.fori_loop(0, 8, body, 0)
-
-    def body_h(k, carry):
+
+    for xp in columns:
+        body(xp)
+
+    def body_h(k):
         xp = k + 1
 
         def halo(u, xq, dy=0):
             p = PACK - 3 * u
             return jnp.where(
-                lane < 3, lroll(strip(3, 7, xq, dy), -p), lroll(strip(3, 6, xq, dy), 125 - p)
+                lane < 3, lroll(strip(Z_TILE, 7, xq, dy), -p), lroll(strip(Z_TILE, 6, xq, dy), 125 - p)
             )
 
         vals = [halo(u, xp) for u in range(9)]
-        first = T[pl.ds(row_of(0, xp + 1, 2) + 7, 8, stride=8), :]
+        inner = T[pl.ds(row_of(0, xp + 1, 2) + 7, 8, stride=8), :]
         upper = [
             halo(5, xp + 1),
             halo(6, xp, 1),
-            lroll(jnp.where(lane == 0, first, vals[7]), 127),
+            lroll(jnp.where(lane == 0, inner, vals[7]), 127),
         ]
         prims, ele = finish(vals[:5], vals[5:8], upper, vals[8], halo(15, xp))
-        at = pl.ds(pl.multiple_of(8 + k * 8, 8), 8)
+        at = aligned(8 + k * 8)
         for q in range(8):
             PH[q, at, :] = prims[q]
         for i in range(3):
             EH[i, at, :] = ele[i]
-        return carry
-
-    lax.fori_loop(0, 6, body_h, 0)
+
+    for k in halo_columns:
+        body_h(k)
 
 
 def limited(a, b):
@@ -294,27 +331,27 @@
     def half(a, b):
         return 0.5 * (a + b)
 
-    def body_x(i, carry):
+    def body_x(i):
         both = [recon(*[prim(q, i + a) for a in (-2, -1, 0, 1)]) for q in range(8)]
         chi = half(strip(1, 0, i - 1), strip(1, 0, i))
         lapse = half(strip(1, 7, i - 1), strip(1, 7, i))
         out = face_flux([b[0] for b in both], [b[1] for b in both], strip(0, 5, i), chi, lapse, 0)
-        at = pl.ds(pl.multiple_of(i * 8, 8), 8)
+        at = aligned(i * 8)
         for q in range(5):
             FX[q, at, :] = out[q]
-        return carry
-
-    lax.fori_loop(0, 5, body_x, 0)
-
-    def body(x, carry):
-        at = pl.ds(pl.multiple_of(x * 8, 8), 8)
-        up = pl.ds(pl.multiple_of(x * 8 + 8, 8), 8)
+
+    for i in range(5):
+        body_x(i)
+
+    def body(x):
+        at = aligned(x * 8)
+        up = aligned(x * 8 + 8)
         chi0, lapse0 = strip(1, 0, x), strip(1, 7, x)
         both = [recon(*[prim(q, x, a) for a in (-2, -1, 0, 1)]) for q in range(8)]
         chi = half(strip(1, 0, x, -1), chi0)
         lapse = half(strip(1, 7, x, -1), lapse0)
         fy = face_flux([b[0] for b in both], [b[1] for b in both], strip(0, 6, x), chi, lapse, 1)
-        zlo, zhi = strip(3, 6, x), strip(3, 7, x)
+        zlo, zhi = strip(Z_TILE, 6, x), strip(Z_TILE, 7, x)
 
         def halo(u):
             p = PACK - 3 * u
@@ -322,7 +359,7 @@
 
         chih, lapseh = halo(8), halo(15)
         own = [prim(q, x) for q in range(8)]
-        hal = [PH[q, pl.ds(pl.multiple_of(8 + (x + 1) * 8, 8), 8), :] for q in range(8)]
+        hal = [PH[q, aligned(8 + (x + 1) * 8), :] for q in range(8)]
         both = [
             recon(
                 shifted(own[q], hal[q], -2, lane),
@@ -358,9 +395,9 @@
             fzu = lroll(jnp.where(lane == 0, fl[q], fz[q]), 127)
             fyu = FX[5 + q, pl.ds(x * 8 + 1, 8), :]
             HR[q, at, :] = (fz[q] - fzu) + (fy[q] - fyu) + (FX[q, at, :] - FX[q, up, :])
-        return carry
-
-    lax.fori_loop(0, 4, body, 0)
+
+    for x in range(4):
+        body(x)
 
 
 def field_stage(EC, EH, EZ, HR):
@@ -428,7 +465,7 @@
         def fold(a, b):
             return jnp.where(low, a, b)
 
-        at = pl.ds(pl.multiple_of(8 * h, 8), 8)
+        at = aligned(8 * h)
 
         def strip(ref, q, pad):
             return fold(
@@ -436,7 +473,8 @@
             )
 
         def g(q, v):
-            return G[pl.ds(((q * 3 + v // 8) * 16 + 8 * h) * 8 + v % 8, 8, stride=8), :]
+            t, s = PLACE[v]
+            return G[pl.ds(((q * 3 + t - 1) * 16 + 8 * h) * 8 + s, 8, stride=8), :]
 
         cur = [o_st[v, at, :] for v in range(22)]
         flu = [o_fl[v, at, :] for v in range(8)]
@@ -659,17 +697,10 @@
     ]
 
 
-def rates(T, scratch, o_st, o_fl, RT):
-    G, PR, PH, EC, EH, FX, HR, EZ = scratch
-    prim_stage(T, PR, PH, EC, EH)
-    flux_stage(T, PR, PH, FX, HR)
-    field_stage(EC, EH, EZ, HR)
-    deriv_stage(T, G)
-    algebra_stage(G, PR, HR, o_st, o_fl, RT)
-
-
 MESH = pl.DeviceIdType.MESH
-N_SLOTS = 29
+PHASES = ((0, 1), (1, 7), (8, 7), (15, 7))
+N_SLOTS = 22
+N_GREETED = 18
 
 
 def wave_stage(own):
@@ -683,69 +714,90 @@
 def load_stage(st, fl, o_st, o_fl, T):
     for u in range(30):
         src, dst, v = (fl, o_fl, u) if u < 8 else (st, o_st, u - 8)
+        t, s = (0, u) if u < 8 else PLACE[v]
         for x in range(4):
             value = src[v, x]
-            T[pl.ds(row_of(u // 8, x + 3, 4) + u % 8, 4, stride=8), :] = value
+            T[pl.ds(row_of(t, x + 3, 4) + s, 4, stride=8), :] = value
             dst[v, pl.ds(4 * x, 4), :] = value
 
 
-def local_stage(o_st, o_fl, zsend, mine):
+def speed_stage(st, mine):
+    top = None
+    for x in range(4):
+
+        def own(u):
+            return st[u - 8, x]
+
+        speed = wave_stage(own)
+        top = speed if top is None else jnp.maximum(top, speed)
+    mine[0] = jnp.max(top, axis=0, keepdims=True)
+
+
+def border_stage(o_st, o_fl, zsend):
     lane = lanes()
 
-    def body(h, top):
+    def body(h, carry):
         at = pl.ds(pl.multiple_of(8 * h, 8), 8)
-
-        def own(u):
-            return o_fl[u, at, :] if u < 8 else o_st[u - 8, at, :]
-
         last = jnp.zeros((8, 128), jnp.float32)
         first = jnp.zeros((8, 128), jnp.float32)
         for u in range(30):
-            p = PACK - 3 * u
+            t, s = (0, u) if u < 8 else PLACE[u - 8]
+            p = PACK - 3 * (8 * t + s)
             here = (lane >= p) & (lane < p + 3)
-            value = own(u)
+            value = o_fl[u, at, :] if u < 8 else o_st[u - 8, at, :]
             first = jnp.where(here, lroll(value, p), first)
             last = jnp.where(here, lroll(value, p - 125), last)
         zsend[0, at, :] = last
         zsend[1, at, :] = first
-        return jnp.maximum(top, wave_stage(own))
-
-    top = lax.fori_loop(0, 2, body, jnp.zeros((8, 128), jnp.float32))
-    mine[0] = jnp.max(top, axis=0, keepdims=True)
+        return carry
+
+    lax.fori_loop(0, 2, body, 0)
 
 
 def halo_rows(zrecv, T):
     for side in range(2):
         for x in range(4):
-            T[pl.ds(row_of(3, x + 3, 4) + 6 + side, 4, stride=8), :] = zrecv[
+            T[pl.ds(row_of(Z_TILE, x + 3, 4) + 6 + side, 4, stride=8), :] = zrecv[
                 side, pl.ds(4 * x, 4), :
             ]
 
 
-def kernel(st, fl, o_st, o_fl, T5, zsend, zrecv, mine, slots, RT, ssem, rsem, msem, *scratch):
+def kernel(st, fl, o_st, o_fl, T5, zsend, zrecv, mine, slots, RT, ssem, rsem, msem, known, *scratch):
     gx, gy, gz = lax.axis_index("gx"), lax.axis_index("gy"), lax.axis_index("gz")
-    hi = gy % 2
+    hi, core = gy & 1, gx & 1
     T = T5.reshape(3840, 128)
 
     def at_x(step):
-        x2 = (hi * 4 + gz + step) % 8
-        return (gx, gy - hi + x2 // 4, x2 % 4)
-
+        x2 = (hi * 4 + gz + step) & 7
+        return (gx, gy - hi + (x2 >> 2), x2 & 3)
+
+    mate = (gx + 1 - 2 * core, gy, gz)
     ring_x = [at_x(k) for k in range(1, 8)]
-    ring_y = [(gx, (gy + 2 * k) % 16, gz) for k in range(1, 8)]
-    ring_z = [((gx + k) % 16, gy, gz) for k in range(1, 16)]
-    x_up, x_dn = ((gx + 1) % 16, gy, gz), ((gx + 15) % 16, gy, gz)
-    z_up, z_dn = (gx, gy, (gz + 1) % 4), (gx, gy, (gz + 3) % 4)
-    partner = at_x(4)
-    onward = (gx, (gy + 2 - 4 * hi + 16) % 16, gz)
+    ring_y = [(gx, (gy + 2 * k) & 15, gz) for k in range(1, 8)]
+    ring_z = [((gx + 2 * k) & 15, gy, gz) for k in range(1, 8)]
+    x_up, x_dn = ((gx + 1) & 15, gy, gz), ((gx + 15) & 15, gy, gz)
+    z_up, z_dn = (gx, gy, (gz + 1) & 3), (gx, gy, (gz + 3) & 3)
+    y_up, y_dn = ring_y[0], ring_y[6]
+    cross = ((gx + 15 + 2 * core) & 15, gy, gz)
+    partner = ring_x[3]
+    onward = (gx, (gy + 2 - 4 * hi) & 15, gz)
 
     barrier = pltpu.get_barrier_semaphore()
-    for peer in ring_x + ring_y + ring_z:
+    for peer in [partner, mate, cross, y_up, y_dn] + ring_x[:3] + ring_x[4:] + ring_z:
         pl.semaphore_signal(barrier, inc=1, device_id=peer, device_id_type=MESH)
+    speed_stage(st, mine)
     load_stage(st, fl, o_st, o_fl, T)
-    local_stage(o_st, o_fl, zsend, mine)
-    pl.semaphore_wait(barrier, N_SLOTS)
-
+    border_stage(o_st, o_fl, zsend)
+    pl.semaphore_wait(barrier, N_GREETED)
+
+    def tell(step):
+        for peer in (y_up, y_dn):
+            pl.semaphore_signal(known.at[step], inc=1, device_id=peer, device_id_type=MESH)
+
+    def told(step):
+        pl.semaphore_wait(known.at[step], 2)
+
+    tell(0)
     started = []
 
     def send(src, dst, peer):
@@ -762,24 +814,25 @@
         started.append(copy)
         return copy
 
-    def share(phase, base, peers):
+    def share(phase, peers):
+        base = PHASES[phase][0]
         for k, peer in enumerate(peers):
             pltpu.make_async_remote_copy(
                 src_ref=mine.at[phase],
                 dst_ref=slots.at[base + k],
                 send_sem=msem.at[phase],
-                recv_sem=msem.at[3 + phase],
+                recv_sem=msem.at[4 + phase],
                 device_id=peer,
                 device_id_type=MESH,
             ).start()
 
-    def gathered(phase, base, count):
-        part = slots.at[pl.ds(base, count)]
-        pltpu.make_async_copy(part, part, msem.at[3 + phase]).wait()
-        mine[phase + 1] = jnp.maximum(mine[phase], jnp.max(slots[pl.ds(base, count)], axis=0))
-
-    def drained(phase, base, count):
-        part = slots.at[pl.ds(base, count)]
+    def gathered(phase):
+        part = slots.at[pl.ds(*PHASES[phase])]
+        pltpu.make_async_copy(part, part, msem.at[4 + phase]).wait()
+        mine[phase + 1] = jnp.maximum(mine[phase], jnp.max(slots[pl.ds(*PHASES[phase])], axis=0))
+
+    def drained(phase):
+        part = slots.at[pl.ds(*PHASES[phase])]
         pltpu.make_async_copy(part, part, msem.at[phase]).wait()
 
     def block(t, n, xp, nx, yp, ny):
@@ -804,50 +857,70 @@
             copies.append(send(block(t, n, 5, 2, yp, 2), block(t, n, 1, 2, yp, 2), x_up))
         return copies
 
+    G, PR, PH, EC, EH, FX, HR, EZ = scratch
+    far, relay, side = {}, {}, {}
+    share(0, [mate])
     zs = [send(zsend.at[0], zrecv.at[0], z_up), send(zsend.at[1], zrecv.at[1], z_dn)]
-    share(0, 0, ring_x)
-    far = [to_partner(t) for t in range(3)]
-    side = faces(0, 3)
+    for t in range(2):
+        far[t] = to_partner(t)
+    front = faces(0, 2)
+    gathered(0)
+    share(1, ring_z)
     for copy in zs:
         copy.wait_recv()
     halo_rows(zrecv, T)
-    far.append(to_partner(3))
-    side += faces(3, 1)
-    gathered(0, 0, 7)
-    share(1, 7, ring_y)
-    relay = []
-    for t in range(2):
-        far[t].wait_recv()
-        relay.append(go_on(t))
-    gathered(1, 7, 7)
-    share(2, 14, ring_z)
-    for t in range(2, 4):
-        far[t].wait_recv()
-        relay.append(go_on(t))
+    for t in (2, 3):
+        far[t] = to_partner(t)
+    front += faces(2, 2)
+    told(0)
+    tell(1)
+    for copy in front:
+        copy.wait_recv()
+    deriv_xz(T, G, (1,))
+    far[0].wait_recv()
+    relay[0] = go_on(0)
+    gathered(1)
+    share(2, ring_x)
+    told(1)
+    tell(2)
+    deriv_xz(T, G, (2,))
+    far[1].wait_recv()
+    relay[1] = go_on(1)
+    far[2].wait_recv()
+    relay[2] = go_on(2)
     for t in range(2):
         relay[t].wait_recv()
-    side += edges(0, 2)
-    for t in range(2, 4):
-        relay[t].wait_recv()
-    side += edges(2, 2)
-    for copy in side:
-        copy.wait_recv()
-
-    rates(T, scratch, o_st, o_fl, RT)
-    gathered(2, 14, 15)
-    step = 0.25 / jnp.max(mine[3], axis=1, keepdims=True)
+        side[t] = edges(t, 1)
+    gathered(2)
+    told(2)
+    share(3, ring_y)
+    far[3].wait_recv()
+    relay[3] = go_on(3)
+    relay[2].wait_recv()
+    side[2] = edges(2, 1)
+    deriv_xz(T, G, (3,))
+    prim_stage(T, PR, PH, EC, EH, (2, 3, 4), (1, 2, 3))
+    deriv_y(T, G, (1, 2))
+    relay[3].wait_recv()
+    deriv_y(T, G, (3,))
+    for t in range(3):
+        for copy in side[t]:
+            copy.wait_recv()
+    deriv_xy(T, G, (1, 2))
+    prim_stage(T, PR, PH, EC, EH, (0, 1, 5, 6, 7), (0, 4, 5))
+    flux_stage(T, PR, PH, FX, HR)
+    field_stage(EC, EH, EZ, HR)
+    algebra_stage(G, PR, HR, o_st, o_fl, RT)
+    gathered(3)
+    step = 0.25 / jnp.max(mine[4], axis=1, keepdims=True)
     for v in range(22):
         o_st[v] = o_st[v] + step * RT[v]
     for v in range(8):
         o_fl[v] = o_fl[v] + step * RT[22 + v]
     for copy in started:
         copy.wait_send()
-    drained(0, 0, 7)
-    drained(1, 7, 7)
-    drained(2, 14, 15)
-
-
-N_COPIES = 2 + 8 + 4 + 8
+    for phase in range(4):
+        drained(phase)
 
 
 def per_device(spacetime, fluid):
@@ -865,15 +938,18 @@
             space(4, PADX, PADY, 8, 128),
             space(2, 16, 128),
             space(2, 16, 128),
-            space(4, 1, 128),
+            space(5, 1, 128),
             space(N_SLOTS, 1, 128),
             space(30, 16, 128),
-            pltpu.SemaphoreType.DMA((30,)),
-            pltpu.SemaphoreType.DMA((30,)),
-            pltpu.SemaphoreType.DMA((6,)),
+            pltpu.SemaphoreType.DMA((32,)),
+            pltpu.SemaphoreType.DMA((32,)),
+            pltpu.SemaphoreType.DMA((8,)),
+            pltpu.SemaphoreType.REGULAR((3,)),
         ]
         + compute_scratch(),
-        compiler_params=pltpu.CompilerParams(collective_id=1, has_side_effects=True),
+        compiler_params=pltpu.CompilerParams(
+            collective_id=1, has_side_effects=True, vmem_limit_bytes=16 << 20
+        ),
     )(spacetime, fluid)
     return st_new.reshape(22, 4, 4, 128), fl_new.reshape(8, 4, 4, 128)
 

time: 58.8 us -> 48.8 us (0.83)
  Pallas kernels: 55.7 us -> 44.9 us
  local copies, waits for them, and re-layouts: 2.27 us -> 3.06 us
    pallas_call x1, Pallas kernels: 55.7 us -> 44.9 us  [per_device(): pl.pallas_call(kernel, out_shape=(jax.ShapeDtypeStruct((22, 16, 128), jnp...]
    unnamed x4 -> x6, local copies, waits for them, and re-layouts: 2.27 us -> 3.06 us
where the time goes in v2:
time: 48.8 us; the launch traced here: 48.6 us
  Pallas kernels  44.9 us (92%)
  local copies, waits for them, and re-layouts  3.06 us (6%)
  between operations  0.65 us (1%)
    pallas_call x1, Pallas kernels, per_device(): pl.pallas_call(kernel, out_shape=(jax.ShapeDtypeStruct((22, 16, 128), jnp...  44.9 us
    unnamed x6, local copies, waits for them, and re-layouts  3.06 us

profile of v2, /device:TPU:3, one launch (start us, length us, event | category | flops | bytes accessed | tf_op | source)
XLA Modules:
  0.0 48.6 jit_solution(4717043545507505510)
XLA Ops:
  0.6 0.0 copy-start
  0.6 0.9 %copy-done = f32[22,4,4,128]{3,2,1,0:T(4,128)S(1)} copy-done((f32[22,4,4,128]{3,2,1,0:T(4,128)S(1)}, f32[22,4,4,128]{3,2,1,0:T(4,128)}, u32[]{:S(2)}) %copy-start) | copy-done | bytes 180248
  1.6 0.0 copy-start.1
  1.6 0.8 %copy-done.1 = f32[8,4,4,128]{3,2,1,0:T(4,128)S(1)} copy-done((f32[8,4,4,128]{3,2,1,0:T(4,128)S(1)}, f32[8,4,4,128]{3,2,1,0:T(4,128)}, u32[]{:S(2)}) %copy-start.1) | copy-done | bytes 65560
  2.4 44.9 %shard_map.41 = (f32[22,16,128]{2,1,0:T(8,128)S(1)}, f32[8,16,128]{2,1,0:T(8,128)S(1)}) custom-call(f32[22,4,4,128]{3,2,1,0:T(4,128)S(1)} %copy-done, f32[8,4,4,128]{3,2,1,0:T(4,128)S(1)} %copy-done.1), custom_call_target="tpu_custom_call" | custom-call | tf_op jit(solution)/shard_map/pallas_call | solution.py:929
  47.3 0.7 %copy.6 = f32[22,4,4,128]{3,2,1,0:T(4,128)} copy(f32[22,4,4,128]{3,2,1,0:T(4,128)S(1)} %bitcast.2) | data formatting | bytes 360448
  47.9 0.6 %copy.7 = f32[8,4,4,128]{3,2,1,0:T(4,128)} copy(f32[8,4,4,128]{3,2,1,0:T(4,128)S(1)} %bitcast.3) | data formatting | bytes 131072
Async XLA Ops:
  0.6 0.9 %copy-start = (f32[22,4,4,128]{3,2,1,0:T(4,128)S(1)}, f32[22,4,4,128]{3,2,1,0:T(4,128)}, u32[]{:S(2)}) copy-start(f32[22,4,4,128]{3,2,1,0:T(4,128)} %st.1) | copy-start | bytes 540676
  1.6 0.8 %copy-start.1 = (f32[8,4,4,128]{3,2,1,0:T(4,128)S(1)}, f32[8,4,4,128]{3,2,1,0:T(4,128)}, u32[]{:S(2)}) copy-start(f32[8,4,4,128]{3,2,1,0:T(4,128)} %fl.1) | copy-start | bytes 196612

commit v3 on v2

--- a/solution.py
+++ b/solution.py
@@ -711,10 +711,12 @@
     return jnp.maximum(jnp.maximum(speeds[0], speeds[1]), speeds[2])
 
 
-def load_stage(st, fl, o_st, o_fl, T):
+def load_stage(st, fl, o_st, o_fl, T, tiles):
     for u in range(30):
         src, dst, v = (fl, o_fl, u) if u < 8 else (st, o_st, u - 8)
         t, s = (0, u) if u < 8 else PLACE[v]
+        if t not in tiles:
+            continue
         for x in range(4):
             value = src[v, x]
             T[pl.ds(row_of(t, x + 3, 4) + s, 4, stride=8), :] = value
@@ -762,7 +764,7 @@
             ]
 
 
-def kernel(st, fl, o_st, o_fl, T5, zsend, zrecv, mine, slots, RT, ssem, rsem, msem, known, *scratch):
+def kernel(st_in, fl_in, o_st, o_fl, st, fl, insem, T5, zsend, zrecv, mine, slots, RT, ssem, rsem, msem, known, *scratch):
     gx, gy, gz = lax.axis_index("gx"), lax.axis_index("gy"), lax.axis_index("gz")
     hi, core = gy & 1, gx & 1
     T = T5.reshape(3840, 128)
@@ -785,8 +787,18 @@
     barrier = pltpu.get_barrier_semaphore()
     for peer in [partner, mate, cross, y_up, y_dn] + ring_x[:3] + ring_x[4:] + ring_z:
         pl.semaphore_signal(barrier, inc=1, device_id=peer, device_id_type=MESH)
+    fetched = [
+        pltpu.make_async_copy(st_in, st, insem.at[0]),
+        pltpu.make_async_copy(fl_in, fl, insem.at[1]),
+    ]
+    for copy in fetched:
+        copy.start()
+    fetched[0].wait()
     speed_stage(st, mine)
-    load_stage(st, fl, o_st, o_fl, T)
+    load_stage(st, fl, o_st, o_fl, T, (1,))
+    fetched[1].wait()
+    load_stage(st, fl, o_st, o_fl, T, (0,))
+    load_stage(st, fl, o_st, o_fl, T, (2, 3))
     border_stage(o_st, o_fl, zsend)
     pl.semaphore_wait(barrier, N_GREETED)
 
@@ -797,7 +809,6 @@
     def told(step):
         pl.semaphore_wait(known.at[step], 2)
 
-    tell(0)
     started = []
 
     def send(src, dst, peer):
@@ -860,17 +871,18 @@
     G, PR, PH, EC, EH, FX, HR, EZ = scratch
     far, relay, side = {}, {}, {}
     share(0, [mate])
+    tell(0)
     zs = [send(zsend.at[0], zrecv.at[0], z_up), send(zsend.at[1], zrecv.at[1], z_dn)]
     for t in range(2):
         far[t] = to_partner(t)
     front = faces(0, 2)
-    gathered(0)
-    share(1, ring_z)
     for copy in zs:
         copy.wait_recv()
     halo_rows(zrecv, T)
     for t in (2, 3):
         far[t] = to_partner(t)
+    gathered(0)
+    share(1, ring_z)
     front += faces(2, 2)
     told(0)
     tell(1)
@@ -932,9 +944,12 @@
             jax.ShapeDtypeStruct((22, 16, 128), jnp.float32),
             jax.ShapeDtypeStruct((8, 16, 128), jnp.float32),
         ),
-        in_specs=[vmem, vmem],
+        in_specs=[pl.BlockSpec(memory_space=pltpu.HBM)] * 2,
         out_specs=(vmem, vmem),
         scratch_shapes=[
+            space(22, 4, 4, 128),
+            space(8, 4, 4, 128),
+            pltpu.SemaphoreType.DMA((2,)),
             space(4, PADX, PADY, 8, 128),
             space(2, 16, 128),
             space(2, 16, 128),
@@ -948,7 +963,7 @@
         ]
         + compute_scratch(),
         compiler_params=pltpu.CompilerParams(
-            collective_id=1, has_side_effects=True, vmem_limit_bytes=16 << 20
+            collective_id=1, has_side_effects=True, vmem_limit_bytes=56164352
         ),
     )(spacetime, fluid)
     return st_new.reshape(22, 4, 4, 128), fl_new.reshape(8, 4, 4, 128)

time: 48.8 us -> 47.9 us (0.982)
  local copies, waits for them, and re-layouts: 3.06 us -> 2.14 us
    unnamed x6 -> x4, local copies, waits for them, and re-layouts: 3.06 us -> 2.14 us
where the time goes in v3:
time: 47.9 us; the launch traced here: 47.6 us
  Pallas kernels  44.9 us (94%)
  local copies, waits for them, and re-layouts  2.14 us (4%)
  between operations  0.65 us (1%)
    pallas_call x1, Pallas kernels, per_device(): pl.pallas_call(kernel, out_shape=(jax.ShapeDtypeStruct((22, 16, 128), jnp...  44.9 us
    unnamed x4, local copies, waits for them, and re-layouts  2.14 us

profile of v3, /device:TPU:3, one launch (start us, length us, event | category | flops | bytes accessed | tf_op | source)
XLA Modules:
  0.0 47.6 jit_solution(17326882749023919483)
XLA Ops:
  0.6 0.0 copy-start
  0.6 0.8 %copy-done = f32[8,4,4,128]{3,2,1,0:T(4,128)S(1)} copy-done((f32[8,4,4,128]{3,2,1,0:T(4,128)S(1)}, f32[8,4,4,128]{3,2,1,0:T(4,128)}, u32[]{:S(2)}) %copy-start) | copy-done | bytes 65560
  1.5 44.9 %shard_map.41 = (f32[22,16,128]{2,1,0:T(8,128)S(1)}, f32[8,16,128]{2,1,0:T(8,128)S(1)}) custom-call(f32[22,4,4,128]{3,2,1,0:T(4,128)} %st_in.1, f32[8,4,4,128]{3,2,1,0:T(4,128)S(1)} %copy-done), custom_call_target="tpu_custom_call" | custom-call | tf_op jit(solution)/shard_map/pallas_call | solution.py:941
  46.3 0.7 %copy.6 = f32[22,4,4,128]{3,2,1,0:T(4,128)} copy(f32[22,4,4,128]{3,2,1,0:T(4,128)S(1)} %bitcast.2) | data formatting | bytes 360448
  47.0 0.6 %copy.7 = f32[8,4,4,128]{3,2,1,0:T(4,128)} copy(f32[8,4,4,128]{3,2,1,0:T(4,128)S(1)} %bitcast.3) | data formatting | bytes 131072
Async XLA Ops:
  0.6 0.8 %copy-start = (f32[8,4,4,128]{3,2,1,0:T(4,128)S(1)}, f32[8,4,4,128]{3,2,1,0:T(4,128)}, u32[]{:S(2)}) copy-start(f32[8,4,4,128]{3,2,1,0:T(4,128)} %fl_in.1) | copy-start | bytes 196612

commit v4 on v3

--- a/solution.py
+++ b/solution.py
@@ -319,7 +319,7 @@
     return m1 + 0.5 * limited(m1 - m2, mid), c0 - 0.5 * limited(mid, p1 - c0)
 
 
-def flux_stage(T, PR, PH, FX, HR):
+def flux_stage(T, PR, PH, FX, HR, columns, last):
     lane = lanes()
 
     def strip(t, s, x, dy=0):
@@ -340,12 +340,11 @@
         for q in range(5):
             FX[q, at, :] = out[q]
 
-    for i in range(5):
+    for i in range(5 if last else 0):
         body_x(i)
 
     def body(x):
         at = aligned(x * 8)
-        up = aligned(x * 8 + 8)
         chi0, lapse0 = strip(1, 0, x), strip(1, 7, x)
         both = [recon(*[prim(q, x, a) for a in (-2, -1, 0, 1)]) for q in range(8)]
         chi = half(strip(1, 0, x, -1), chi0)
@@ -394,10 +393,14 @@
         for q in range(5):
             fzu = lroll(jnp.where(lane == 0, fl[q], fz[q]), 127)
             fyu = FX[5 + q, pl.ds(x * 8 + 1, 8), :]
-            HR[q, at, :] = (fz[q] - fzu) + (fy[q] - fyu) + (FX[q, at, :] - FX[q, up, :])
-
-    for x in range(4):
+            HR[q, at, :] = (fz[q] - fzu) + (fy[q] - fyu)
+
+    for x in columns:
         body(x)
+    if last:
+        low, high = pl.ds(0, 32), pl.ds(8, 32)
+        for q in range(5):
+            HR[q, low, :] = HR[q, low, :] + (FX[q, low, :] - FX[q, high, :])
 
 
 def field_stage(EC, EH, EZ, HR):
@@ -886,20 +889,19 @@
     front += faces(2, 2)
     told(0)
     tell(1)
-    for copy in front:
-        copy.wait_recv()
-    deriv_xz(T, G, (1,))
     far[0].wait_recv()
     relay[0] = go_on(0)
     gathered(1)
     share(2, ring_x)
     told(1)
     tell(2)
-    deriv_xz(T, G, (2,))
     far[1].wait_recv()
     relay[1] = go_on(1)
     far[2].wait_recv()
     relay[2] = go_on(2)
+    for copy in front:
+        copy.wait_recv()
+    deriv_xz(T, G, (1, 2, 3))
     for t in range(2):
         relay[t].wait_recv()
         side[t] = edges(t, 1)
@@ -910,17 +912,16 @@
     relay[3] = go_on(3)
     relay[2].wait_recv()
     side[2] = edges(2, 1)
-    deriv_xz(T, G, (3,))
     prim_stage(T, PR, PH, EC, EH, (2, 3, 4), (1, 2, 3))
-    deriv_y(T, G, (1, 2))
+    flux_stage(T, PR, PH, FX, HR, (0, 1, 2), False)
     relay[3].wait_recv()
-    deriv_y(T, G, (3,))
+    deriv_y(T, G, (1, 2, 3))
     for t in range(3):
         for copy in side[t]:
             copy.wait_recv()
     deriv_xy(T, G, (1, 2))
     prim_stage(T, PR, PH, EC, EH, (0, 1, 5, 6, 7), (0, 4, 5))
-    flux_stage(T, PR, PH, FX, HR)
+    flux_stage(T, PR, PH, FX, HR, (3,), True)
     field_stage(EC, EH, EZ, HR)
     algebra_stage(G, PR, HR, o_st, o_fl, RT)
     gathered(3)

time: 47.9 us -> 47.4 us (0.990)
  Pallas kernels: 44.9 us -> 44.4 us
where the time goes in v4:
time: 47.4 us; the launch traced here: 47.2 us
  Pallas kernels  44.4 us (94%)
  local copies, waits for them, and re-layouts  2.14 us (5%)
  between operations  0.65 us (1%)
    pallas_call x1, Pallas kernels, per_device(): pl.pallas_call(kernel, out_shape=(jax.ShapeDtypeStruct((22, 16, 128), jnp...  44.4 us
    unnamed x4, local copies, waits for them, and re-layouts  2.14 us

profile of v4, /device:TPU:3, one launch (start us, length us, event | category | flops | bytes accessed | tf_op | source)
XLA Modules:
  0.0 47.2 jit_solution(3531078972228187136)
XLA Ops:
  0.6 0.0 copy-start
  0.6 0.8 %copy-done = f32[8,4,4,128]{3,2,1,0:T(4,128)S(1)} copy-done((f32[8,4,4,128]{3,2,1,0:T(4,128)S(1)}, f32[8,4,4,128]{3,2,1,0:T(4,128)}, u32[]{:S(2)}) %copy-start) | copy-done | bytes 65560
  1.5 44.4 %shard_map.41 = (f32[22,16,128]{2,1,0:T(8,128)S(1)}, f32[8,16,128]{2,1,0:T(8,128)S(1)}) custom-call(f32[22,4,4,128]{3,2,1,0:T(4,128)} %st_in.1, f32[8,4,4,128]{3,2,1,0:T(4,128)S(1)} %copy-done), custom_call_target="tpu_custom_call" | custom-call | tf_op jit(solution)/shard_map/pallas_call | solution.py:942
  45.9 0.7 %copy.6 = f32[22,4,4,128]{3,2,1,0:T(4,128)} copy(f32[22,4,4,128]{3,2,1,0:T(4,128)S(1)} %bitcast.2) | data formatting | bytes 360448
  46.6 0.6 %copy.7 = f32[8,4,4,128]{3,2,1,0:T(4,128)} copy(f32[8,4,4,128]{3,2,1,0:T(4,128)S(1)} %bitcast.3) | data formatting | bytes 131072
Async XLA Ops:
  0.6 0.8 %copy-start = (f32[8,4,4,128]{3,2,1,0:T(4,128)S(1)}, f32[8,4,4,128]{3,2,1,0:T(4,128)}, u32[]{:S(2)}) copy-start(f32[8,4,4,128]{3,2,1,0:T(4,128)} %fl_in.1) | copy-start | bytes 196612
